TPU v7x, 256 devices: a whole 4x4x8 slice. The times are simulated.
256 devices in a mesh: gx: 16 (over y, z_hi, core), gy: 16 (over z_lo, x).
Axes of the slice: x: 4, y: 4, z: 8 (z_hi: 2, z_lo: 4; z = z_hi * 4 + z_lo), core: 2. Of those that a mesh axis runs over, the one named last changes fastest.
Arguments:
- pressure: float32 [512, 512, 128], P('gx', 'gy'), may hold values from -6 to 6
- vel_x: float32 [512, 512, 128], P('gx', 'gy'), may hold values from -6 to 6
- vel_y: float32 [512, 512, 128], P('gx', 'gy'), may hold values from -6 to 6
- vel_z: float32 [512, 512, 128], P('gx', 'gy'), may hold values from -6 to 6
- material: int32 [512, 512, 128], P('gx', 'gy'), may hold values from 0 to 3
- density_table: float32 [4], replicated, may hold values from 0.5 to 4
- speed_table: float32 [4], replicated, may hold values from 0.3 to 1
- panel_vals: float32 [512, 128, 8, 128], P(('gx', 'gy')), may hold values from -6 to 6
- panel_tile: int32 [512, 128, 1], P(('gx', 'gy')), may hold values from 0 to 255; in each aligned block of 256 rows (0 to 255, 256 to 511, ..., all dimensions but the last counted through in order) at most 2 rows name the same one
- panel_cell: int32 [512, 128], P(('gx', 'gy')), may hold values from 0 to 1023
Outputs:
- pressure_out: float32 [512, 512, 128], P('gx', 'gy')
- vel_x_out: float32 [512, 512, 128], P('gx', 'gy')
- vel_y_out: float32 [512, 512, 128], P('gx', 'gy')
- vel_z_out: float32 [512, 512, 128], P('gx', 'gy')
Inputs may be any that keep to these rules, and one draw needn't show every extreme that they name: `panel_tile`: among the 256 columns of the panels of one device, no tile is named more than 2 times, a bound that some block reaches.
All inputs are finite; a program needn't handle non-finite values.
Results may differ from a plain program's by a relative error of at most 0.00002.
Values sent between devices are 32-bit elements; how exact they have to be, the bound alone decides.
No kernel may reach another device: no remote copies, remote signals or barrier semaphores. Data moves between devices by JAX's collectives and lax.ppermute only.
A program may use at most 64 MiB of HBM per device.

v0:
```python
import jax
import jax.numpy as jnp
from jax import lax
from jax.experimental import pallas as pl
from jax.experimental.pallas import tpu as pltpu
from jax.sharding import PartitionSpec as P

courant = 0.55
STEPS = 8
DEPTH = 8
LAST = STEPS - 1
X_START = [sum(LAST - t for t in range(s)) for s in range(STEPS)]
X_PLANES = X_START[LAST]
PAIRS = 4
Y_REACH = [LAST - 1 - q for q in range(PAIRS)]
VMEM = pl.BlockSpec(memory_space=pltpu.VMEM)
SMEM = pl.BlockSpec(memory_space=pltpu.SMEM)


def call(kernel, outs, in_specs, micros, mib, scratch=()):
    return pl.pallas_call(
        kernel,
        out_shape=[jax.ShapeDtypeStruct(shape, jnp.float32) for shape in outs],
        in_specs=in_specs,
        out_specs=[VMEM] * len(outs),
        scratch_shapes=list(scratch),
        compiler_params=pltpu.CompilerParams(vmem_limit_bytes=mib << 20),
        cost_estimate=pl.CostEstimate(
            flops=0, transcendentals=0, bytes_accessed=int(micros * 2_000_000)
        ),
    )


def moved(block, axis, distance):
    devices = range(lax.axis_size(axis))
    route = [(i - distance, i) for i in devices if i - distance in devices]
    return lax.ppermute(block, axis, route)


def pack_kernel(p, vx, vy, vz, mat, first, last):
    wide = p.shape[0]
    for a, ref in enumerate((p, vx, vy, vz)):
        first[a] = ref[:DEPTH]
        last[a] = ref[wide - DEPTH :]
    first[4] = mat[:DEPTH].astype(jnp.float32) + 1.0
    last[4] = mat[wide - DEPTH :].astype(jnp.float32) + 1.0


def send_kernel(tile, rank, cell, vals, out):
    block = 2 * STEPS + 1
    tiles = out.shape[0] // block
    zero = jnp.zeros((16, out.shape[1]), jnp.float32)
    lane = lax.broadcasted_iota(jnp.int32, (1, out.shape[1]), 1)

    def clear(i, c):
        for u in range(4):
            out[pl.ds(pl.multiple_of(i * 64 + u * 16, 16), 16), :] = zero
        return c

    lax.fori_loop(0, out.shape[0] // 64, clear, 0)
    out[pl.ds(2 * STEPS, tiles, stride=block), :] = jnp.full((tiles, out.shape[1]), 65536.0)

    def place(i, c):
        for u in range(8):
            k = i * 8 + u
            at = tile[k] * block
            slot = rank[k]
            out[pl.ds(at + slot * STEPS, STEPS), :] = vals[k]
            named = out[pl.ds(at + 2 * STEPS, 1), :]
            own = cell[k].astype(jnp.float32)
            out[pl.ds(at + 2 * STEPS, 1), :] = jnp.where(lane == slot, own, named)
        return c

    lax.fori_loop(0, vals.shape[0] // 8, place, 0)


def edge_kernel(p, vx, vy, vz, mat, low, high, first, last):
    wide, tall = p.shape[:2]
    for a, ref in enumerate((p, vx, vy, vz, mat)):
        for out, rows in ((first, slice(0, 8)), (last, slice(tall - 8, tall))):
            out[a, :DEPTH] = low[a, :, rows, :]
            inner = ref[:, rows, :]
            if a == 4:
                inner = inner.astype(jnp.float32) + 1.0
            out[a, DEPTH : DEPTH + wide] = inner
            out[a, DEPTH + wide :] = high[a, :, rows, :]


def extend_kernel(btab, stab, p, vx, vy, vz, mat, low, high, ylow, yhigh, *outs):
    wide, _ = p.shape[:2]

    def put(x, a, parts):
        full = jnp.concatenate(parts, axis=0)
        if a < 4:
            outs[a][x] = full
            return
        b = jnp.zeros_like(full)
        s = jnp.zeros_like(full)
        for m in range(btab.shape[0]):
            b = jnp.where(full == float(m + 1), btab[m], b)
            s = jnp.where(full == float(m + 1), stab[m], s)
        outs[4][x] = b
        outs[5][x] = s

    for a, ref in enumerate((p, vx, vy, vz, mat)):

        def lower(i, c):
            put(i, a, [ylow[a, i], low[a, i], yhigh[a, i]])
            return c

        def inner(i, c):
            mid = ref[i]
            if a == 4:
                mid = mid.astype(jnp.float32) + 1.0
            put(i + DEPTH, a, [ylow[a, i + DEPTH], mid, yhigh[a, i + DEPTH]])
            return c

        def upper(i, c):
            x = i + DEPTH + wide
            put(x, a, [ylow[a, x], high[a, i], yhigh[a, x]])
            return c

        lax.fori_loop(0, DEPTH, lower, 0)
        lax.fori_loop(0, wide, inner, 0)
        lax.fori_loop(0, DEPTH, upper, 0)


def thirds(v):
    hi = v.astype(jnp.bfloat16)
    rest = v - hi.astype(jnp.float32)
    mid = rest.astype(jnp.bfloat16)
    return hi, mid, (rest - mid.astype(jnp.float32)).astype(jnp.bfloat16)


def one_hot(cells, base, count):
    ids = lax.broadcasted_iota(jnp.int32, (count, cells.shape[1]), 0) + base
    return jnp.where(ids.astype(jnp.float32) == cells, 1.0, 0.0).astype(jnp.bfloat16)


def spread(hot, parts):
    total = jnp.dot(hot, parts[0], preferred_element_type=jnp.float32)
    total = total + jnp.dot(hot, parts[1], preferred_element_type=jnp.float32)
    return total + jnp.dot(hot, parts[2], preferred_element_type=jnp.float32)


def source_kernel(arrived, src, first, last, parts_ref):
    block = 2 * STEPS + 1
    tiles = arrived.shape[0] // block
    wide, tall, layers = src.shape[1:]
    named = jnp.transpose(arrived[pl.ds(2 * STEPS, tiles, stride=block), :])
    cells = jnp.concatenate([named[0:1], named[1:2]], axis=1)
    for s in range(STEPS):
        for r in range(2):
            rows = pl.ds(r * STEPS + s, tiles, stride=block)
            for n, part in enumerate(thirds(arrived[rows, :])):
                parts_ref[n, r * tiles : (r + 1) * tiles, s * layers : (s + 1) * layers] = part
    chunk = 8

    def body(i, c):
        hot = one_hot(cells, i * (chunk * tall), chunk * tall)
        for s in range(0, STEPS, 2):
            span = slice(s * layers, (s + 2) * layers)
            got = spread(hot, [parts_ref[n, :, span] for n in range(3)])
            for m in range(2):
                piece = got[:, m * layers : (m + 1) * layers]
                src[s + m, pl.ds(i * chunk, chunk)] = piece.reshape(chunk, tall, layers)
        return c

    lax.fori_loop(0, wide // chunk, body, 0)
    for s in range(LAST):
        for d in range(1, LAST - s + 1):
            first[X_START[s] + d - 1] = src[s, d - 1]
            last[X_START[s] + d - 1] = src[s, wide - d]


def y_start(q, wide):
    return sum(wide + 2 * Y_REACH[t] for t in range(q))


def source_edge_kernel(src, low, high, first, last):
    wide, tall, layers = src.shape[1:]
    row = lax.broadcasted_iota(jnp.int32, (8, layers), 0)
    for q in range(PAIRS):
        near, far, reach = q, LAST - 1 - q, Y_REACH[q]
        base = y_start(q, wide)

        def pack(out, slot, a, b, is_first):
            if b is None:
                out[slot] = a
            elif is_first:
                out[slot] = jnp.where(row <= LAST - 1 - q, a, pltpu.roll(b, LAST - q, 0))
            else:
                out[slot] = jnp.where(row >= q + 1, a, pltpu.roll(b, q + 1, 0))

        for out, at, is_first in ((first, 0, True), (last, tall - 8, False)):
            rows = slice(at, at + 8)

            def inner(i, c):
                for u in range(4):
                    x = i * 4 + u
                    b = src[far, x, rows, :] if far != near else None
                    pack(out, base + reach + x, src[near, x, rows, :], b, is_first)
                return c

            lax.fori_loop(0, wide // 4, inner, 0)
            for d in range(1, reach + 1):
                with_far = far != near and d <= q
                for halo, slot in ((low, base + reach - d), (high, base + reach + wide + d - 1)):
                    a = halo[X_START[near] + d - 1, rows, :]
                    b = halo[X_START[far] + d - 1, rows, :] if with_far else None
                    pack(out, slot, a, b, is_first)


def step_kernel(
    p0, vx0, vy0, vz0, bb, ss, src, low, high, ylow, yhigh,
    p_out, vx_out, vy_out, vz_out, p, vx, vy, vz,
):
    wide, tall, layers = p_out.shape
    full = tall + 2 * DEPTH
    lane = lax.broadcasted_iota(jnp.int32, (full, layers), 1)
    blank = jnp.zeros((8, layers), jnp.float32)

    for s in range(STEPS):
        depth = LAST - s
        p_in, vx_in, vy_in, vz_in = (p0, vx0, vy0, vz0) if s == 0 else (p, vx, vy, vz)
        q = min(s, LAST - 1 - s)

        def tiles(x):
            slot = y_start(q, wide) + Y_REACH[q] + x
            lo, hi = ylow[slot], yhigh[slot]
            if s > LAST - 1 - s:
                lo, hi = pltpu.roll(lo, LAST - q, 0), pltpu.roll(hi, q + 1, 0)
            return lo, hi

        def row(i, carry, source):
            p_cur, vx_prev = carry
            p_next = p_in[i + 1]
            b = bb[i]
            vx_new = vx_in[i] - b * (p_next - p_cur)
            vy_new = vy_in[i] - b * (pltpu.roll(p_cur, full - 1, 0) - p_cur)
            up = jnp.where(lane == layers - 1, 0.0, pltpu.roll(p_cur, layers - 1, 1))
            vz_new = vz_in[i] - b * (up - p_cur)
            down = jnp.where(lane == 0, 0.0, pltpu.roll(vz_new, 1, 1))
            div = (vx_new - vx_prev) + (vy_new - pltpu.roll(vy_new, 1, 0)) + (vz_new - down)
            p_new = p_cur + ss[i] * (source - div)
            if s == LAST:
                keep = slice(DEPTH, DEPTH + tall)
                p_out[i - DEPTH] = p_new[keep]
                vx_out[i - DEPTH] = vx_new[keep]
                vy_out[i - DEPTH] = vy_new[keep]
                vz_out[i - DEPTH] = vz_new[keep]
            else:
                p[i] = p_new
                vx[i] = vx_new
                vy[i] = vy_new
                vz[i] = vz_new
            return p_next, vx_new

        begin = DEPTH - depth
        p_cur = p_in[begin]
        before = p_in[begin - 1]
        carry = (p_cur, vx_in[begin - 1] - bb[begin - 1] * (p_cur - before))
        for d in range(depth, 0, -1):
            lo, hi = tiles(-d) if d < depth else (blank, blank)
            source = jnp.concatenate([lo, low[X_START[s] + d - 1], hi], axis=0)
            carry = row(DEPTH - d, carry, source)

        def inner(n, carry):
            for u in range(4):
                i = n * 4 + u
                if s == LAST:
                    source = jnp.concatenate([blank, src[s, i], blank], axis=0)
                else:
                    lo, hi = tiles(i)
                    source = jnp.concatenate([lo, src[s, i], hi], axis=0)
                carry = row(i + DEPTH, carry, source)
            return carry

        carry = lax.fori_loop(0, wide // 4, inner, carry)
        for d in range(1, depth + 1):
            lo, hi = tiles(wide + d - 1) if d < depth else (blank, blank)
            source = jnp.concatenate([lo, high[X_START[s] + d - 1], hi], axis=0)
            carry = row(DEPTH + wide + d - 1, carry, source)


def program(
    pressure, vel_x, vel_y, vel_z, material, density_table, speed_table,
    panel_vals, panel_tile, panel_cell,
):
    devices = lax.axis_size("gx") * lax.axis_size("gy")
    wide, tall, layers = pressure.shape
    columns = panel_vals.shape[0] * panel_vals.shape[1]
    target = panel_tile.reshape(-1)
    order = jnp.arange(columns, dtype=jnp.int32)
    earlier = (target[:, None] == target[None, :]) & (order[None, :] < order[:, None])
    rank = jnp.sum(earlier.astype(jnp.int32), axis=1)
    values = panel_vals.reshape(columns, STEPS, layers)
    state = (pressure, vel_x, vel_y, vel_z, material)

    first, last = call(pack_kernel, [(5, DEPTH, tall, layers)] * 2, [VMEM] * 5, 1, 8)(*state)
    low, high = moved(last, "gx", 1), moved(first, "gx", -1)
    block = 2 * STEPS + 1
    (outgoing,) = call(
        send_kernel, [(devices * block, layers)], [SMEM] * 3 + [VMEM], 3, 12
    )(target, rank, panel_cell.reshape(-1), values)
    arrived = lax.all_to_all(
        outgoing.reshape(devices, block, 1, layers),
        ("gx", "gy"),
        split_axis=0,
        concat_axis=0,
        tiled=True,
    ).reshape(devices * block, layers)
    y_first, y_last = call(
        edge_kernel, [(5, wide + 2 * DEPTH, 8, layers)] * 2, [VMEM] * 7, 2, 12
    )(*state, low, high)
    y_low, y_high = moved(y_last, "gy", 1), moved(y_first, "gy", -1)
    b_table = courant * (1.0 / density_table)
    s_table = courant * (density_table * speed_table * speed_table)
    box = (wide + 2 * DEPTH, tall + 2 * DEPTH, layers)
    extended = call(extend_kernel, [box] * 6, [SMEM] * 2 + [VMEM] * 9, 4, 20)(
        b_table, s_table, *state, low, high, y_low, y_high
    )

    src, s_first, s_last = call(
        source_kernel,
        [(STEPS, wide, tall, layers)] + [(X_PLANES, tall, layers)] * 2,
        [VMEM],
        5,
        26,
        [pltpu.VMEM((3, 2 * devices, STEPS * layers), jnp.bfloat16)],
    )(arrived)
    s_low, s_high = moved(s_last, "gx", 1), moved(s_first, "gx", -1)
    tiles = y_start(PAIRS, wide)
    e_first, e_last = call(
        source_edge_kernel, [(tiles, 8, layers)] * 2, [VMEM] * 3, 2, 12
    )(src, s_low, s_high)
    e_low, e_high = moved(e_last, "gy", 1), moved(e_first, "gy", -1)

    return tuple(
        call(
            step_kernel,
            [(wide, tall, layers)] * 4,
            [VMEM] * 11,
            12,
            32,
            [pltpu.VMEM(box, jnp.float32)] * 4,
        )(*extended, src, s_low, s_high, e_low, e_high)
    )


def solution(mesh):
    tile = P("gx", "gy", None)
    return jax.shard_map(
        program,
        mesh=mesh,
        in_specs=(tile,) * 5
        + (
            P(),
            P(),
            P(("gx", "gy"), None, None, None),
            P(("gx", "gy"), None, None),
            P(("gx", "gy"), None),
        ),
        out_specs=(tile,) * 4,
        check_vma=False,
    )
```

profile of v0, /device:TPU:87, one launch (start us, length us, event | category | flops | bytes accessed | tf_op | source)
XLA Modules:
  0.0 191.2 jit_solution(16328492170752221071)
XLA Ops:
  0.6 0.9 convert_reduce_fusion.rank
  1.6 1.2 copy-done.9
  2.8 0.7 copy-done.10
  3.5 0.7 copy-done.11
  4.2 2.3 %shard_map.132 = f32[4352,128]{1,0:T(8,128)S(1)} custom-call(s32[256]{0:T(256)S(1)} %bitcast.9, s32[256]{0:T(256)S(1)} %convert_reduce_fusion.rank, s32[256]{0:T(256)S(1)} %bitcast.10, f32[256,8,128]{2,1,0:T(8,128)S(1)} %bitcast.7), custom_call_target="tpu_custom_call" | custom-call | bytes 6000000 | tf_op jit(solution)/shard_map/pallas_call | solution.py:303
  6.5 1.4 copy-done
  7.8 14.4 %all-to-all-start = ((f32[256,17,1,128]{3,2,1,0:T(1,128)}), f32[256,17,1,128]{3,2,1,0:T(1,128)S(1)}, u32[]{:S(2)}, u32[]{:S(2)}) async-start(f32[256,17,1,128]{3,2,1,0:T(1,128)} %bitcast.6), calls=%async_computation | async-start | bytes 4456448 | tf_op jit(solution)/shard_map/all_to_all | solution.py:306
  22.2 0.0 copy-start.3
  22.2 1.0 copy-done.3
  23.3 1.0 copy-done.5
  24.3 1.0 copy-done.7
  25.4 1.1 shard_map.129
  26.5 6.5 %collective-permute-start = (f32[5,8,32,128]{3,2,1,0:T(8,128)}, f32[5,8,32,128]{3,2,1,0:T(8,128)}, u32[]{:S(2)}, u32[]{:S(2)}) collective-permute-start(f32[5,8,32,128]{3,2,1,0:T(8,128)} %get-tuple-element.19), channel_id=1, source_target_pairs={{0,16},{16,32},{32,48},{48,64},{64,80},{80,96},{96,112},{112,128},... | collective-permute-start | bytes 1966088 | tf_op jit(solution)/shard_map/ppermute | solution.py:37
  33.0 1.9 %collective-permute-start.1 = (f32[5,8,32,128]{3,2,1,0:T(8,128)}, f32[5,8,32,128]{3,2,1,0:T(8,128)}, u32[]{:S(2)}, u32[]{:S(2)}) collective-permute-start(f32[5,8,32,128]{3,2,1,0:T(8,128)} %get-tuple-element.20), channel_id=1, source_target_pairs={{16,0},{32,16},{48,32},{64,48},{80,64},{96,80},{112,96},{128,112},... | collective-permute-start | bytes 1966088 | tf_op jit(solution)/shard_map/ppermute | solution.py:37
  35.0 43.8 %all-to-all-done = f32[256,17,1,128]{3,2,1,0:T(1,128)S(1)} async-done(((f32[256,17,1,128]{3,2,1,0:T(1,128)}), f32[256,17,1,128]{3,2,1,0:T(1,128)S(1)}, u32[]{:S(2)}, u32[]{:S(2)}) %all-to-all-start) | async-done | bytes 2228256 | tf_op jit(solution)/shard_map/all_to_all | solution.py:306
  78.8 5.3 %shard_map.133 = (f32[8,32,32,128]{3,2,1,0:T(8,128)S(1)}, f32[28,32,128]{2,1,0:T(8,128)S(1)}, f32[28,32,128]{2,1,0:T(8,128)S(1)}) custom-call(f32[4352,128]{1,0:T(8,128)S(1)} %bitcast.5), custom_call_target="tpu_custom_call" | custom-call | bytes 10000000 | tf_op jit(solution)/shard_map/pallas_call | solution.py:324
  84.1 35.2 %collective-permute-start.4 = (f32[28,32,128]{2,1,0:T(8,128)S(1)}, f32[28,32,128]{2,1,0:T(8,128)S(1)}, u32[]{:S(2)}, u32[]{:S(2)}) collective-permute-start(f32[28,32,128]{2,1,0:T(8,128)S(1)} %get-tuple-element.30), channel_id=1, source_target_pairs={{0,16},{16,32},{32,48},{48,64},{64,80},{80,96},{96,112},{112,128},... | collective-permute-start | bytes 1376264 | tf_op jit(solution)/shard_map/ppermute | solution.py:37
  119.3 1.9 %collective-permute-start.5 = (f32[28,32,128]{2,1,0:T(8,128)S(1)}, f32[28,32,128]{2,1,0:T(8,128)S(1)}, u32[]{:S(2)}, u32[]{:S(2)}) collective-permute-start(f32[28,32,128]{2,1,0:T(8,128)S(1)} %get-tuple-element.31), channel_id=1, source_target_pairs={{16,0},{32,16},{48,32},{64,48},{80,64},{96,80},{112,96},{128,112},... | collective-permute-start | bytes 1376264 | tf_op jit(solution)/shard_map/ppermute | solution.py:37
  121.3 1.4 shard_map.130
  122.7 4.4 %collective-permute-start.2 = (f32[5,48,8,128]{3,2,1,0:T(8,128)S(1)}, f32[5,48,8,128]{3,2,1,0:T(8,128)S(1)}, u32[]{:S(2)}, u32[]{:S(2)}) collective-permute-start(f32[5,48,8,128]{3,2,1,0:T(8,128)S(1)} %get-tuple-element.21), channel_id=1, source_target_pairs={{0,1},{1,2},{2,3},{3,4},{4,5},{5,6},{6,7},{7,8},{8,9},{9,10},{10,1... | collective-permute-start | bytes 2949128 | tf_op jit(solution)/shard_map/ppermute | solution.py:37
  127.1 1.9 %collective-permute-start.3 = (f32[5,48,8,128]{3,2,1,0:T(8,128)S(1)}, f32[5,48,8,128]{3,2,1,0:T(8,128)S(1)}, u32[]{:S(2)}, u32[]{:S(2)}) collective-permute-start(f32[5,48,8,128]{3,2,1,0:T(8,128)S(1)} %get-tuple-element.22), channel_id=1, source_target_pairs={{1,0},{2,1},{3,2},{4,3},{5,4},{6,5},{7,6},{8,7},{9,8},{10,9},{11,1... | collective-permute-start | bytes 2949128 | tf_op jit(solution)/shard_map/ppermute | solution.py:37
  129.0 3.4 %collective-permute-done.4.low = f32[28,32,128]{2,1,0:T(8,128)S(1)} collective-permute-done((f32[28,32,128]{2,1,0:T(8,128)S(1)}, f32[28,32,128]{2,1,0:T(8,128)S(1)}, u32[]{:S(2)}, u32[]{:S(2)}) %collective-permute-start.4) | collective-permute-done | bytes 458784 | tf_op jit(solution)/shard_map/ppermute | solution.py:37
  132.4 7.6 %collective-permute-done.5.high = f32[28,32,128]{2,1,0:T(8,128)S(1)} collective-permute-done((f32[28,32,128]{2,1,0:T(8,128)S(1)}, f32[28,32,128]{2,1,0:T(8,128)S(1)}, u32[]{:S(2)}, u32[]{:S(2)}) %collective-permute-start.5) | collective-permute-done | bytes 458784 | tf_op jit(solution)/shard_map/ppermute | solution.py:37
  140.0 0.5 shard_map.134
  140.5 1.9 %collective-permute-start.6 = (f32[164,8,128]{2,1,0:T(8,128)S(1)}, f32[164,8,128]{2,1,0:T(8,128)S(1)}, u32[]{:S(2)}, u32[]{:S(2)}) collective-permute-start(f32[164,8,128]{2,1,0:T(8,128)S(1)} %get-tuple-element.32), channel_id=1, source_target_pairs={{0,1},{1,2},{2,3},{3,4},{4,5},{5,6},{6,7},{7,8},{8,9},{9,10},{10,1... | collective-permute-start | bytes 2015240 | tf_op jit(solution)/shard_map/ppermute | solution.py:37
  142.4 3.4 %collective-permute-start.7 = (f32[164,8,128]{2,1,0:T(8,128)S(1)}, f32[164,8,128]{2,1,0:T(8,128)S(1)}, u32[]{:S(2)}, u32[]{:S(2)}) collective-permute-start(f32[164,8,128]{2,1,0:T(8,128)S(1)} %get-tuple-element.33), channel_id=1, source_target_pairs={{1,0},{2,1},{3,2},{4,3},{5,4},{6,5},{7,6},{8,7},{9,8},{10,9},{11,1... | collective-permute-start | bytes 2015240 | tf_op jit(solution)/shard_map/ppermute | solution.py:37
  145.8 8.2 %collective-permute-done.2.ylow = f32[5,48,8,128]{3,2,1,0:T(8,128)S(1)} collective-permute-done((f32[5,48,8,128]{3,2,1,0:T(8,128)S(1)}, f32[5,48,8,128]{3,2,1,0:T(8,128)S(1)}, u32[]{:S(2)}, u32[]{:S(2)}) %collective-permute-start.2) | collective-permute-done | bytes 983072 | tf_op jit(solution)/shard_map/ppermute | solution.py:37
  154.0 8.6 %collective-permute-done.3.yhigh = f32[5,48,8,128]{3,2,1,0:T(8,128)S(1)} collective-permute-done((f32[5,48,8,128]{3,2,1,0:T(8,128)S(1)}, f32[5,48,8,128]{3,2,1,0:T(8,128)S(1)}, u32[]{:S(2)}, u32[]{:S(2)}) %collective-permute-start.3) | collective-permute-done | bytes 983072 | tf_op jit(solution)/shard_map/ppermute | solution.py:37
  162.6 3.5 %shard_map.131 = (f32[48,48,128]{2,1,0:T(8,128)S(1)}, f32[48,48,128]{2,1,0:T(8,128)S(1)}, f32[48,48,128]{2,1,0:T(8,128)S(1)}, f32[48,48,128]{2,1,0:T(8,128)S(1)}...) custom-call(f32[4]{0:T(128)S(1)} %get-tuple-element.35.btab, f32[4]{0:T(128)S(1)} %get-tuple-element.34.stab, ...), custom_call_target="tpu_custom_call" | custom-call | bytes 8000000 | tf_op jit(solution)/shard_map/pallas_call | solution.py:320
  166.1 2.3 %collective-permute-done.6.ylow = f32[164,8,128]{2,1,0:T(8,128)S(1)} collective-permute-done((f32[164,8,128]{2,1,0:T(8,128)S(1)}, f32[164,8,128]{2,1,0:T(8,128)S(1)}, u32[]{:S(2)}, u32[]{:S(2)}) %collective-permute-start.6) | collective-permute-done | bytes 671776 | tf_op jit(solution)/shard_map/ppermute | solution.py:37
  168.4 8.6 %collective-permute-done.7.yhigh = f32[164,8,128]{2,1,0:T(8,128)S(1)} collective-permute-done((f32[164,8,128]{2,1,0:T(8,128)S(1)}, f32[164,8,128]{2,1,0:T(8,128)S(1)}, u32[]{:S(2)}, u32[]{:S(2)}) %collective-permute-start.7) | collective-permute-done | bytes 671776 | tf_op jit(solution)/shard_map/ppermute | solution.py:37
  177.0 14.2 %shard_map.135 = (f32[32,32,128]{2,1,0:T(8,128)}, f32[32,32,128]{2,1,0:T(8,128)}, f32[32,32,128]{2,1,0:T(8,128)}, f32[32,32,128]{2,1,0:T(8,128)}) custom-call(f32[48,48,128]{2,1,0:T(8,128)S(1)} %get-tuple-element.23.p0, f32[48,48,128]{2,1,0:T(8,128)S(1)} %get-tuple-element.24.vx0, f32[48,48,128]{2,1,0:T(8,128)S(1)} %get-tuple-element.25.vy0, ...), custom_call_target="tpu_custom_call" | custom-call | bytes 24000000 | tf_op jit(solution)/shard_map/pallas_call | solution.py:340
  (23 shorter events, 0.1 us)
Async XLA Ops:
  1.6 1.2 copy-start.9
  2.8 0.7 copy-start.10
  3.5 0.7 copy-start.11
  6.5 1.4 copy-start
  7.8 14.4 %copy-start.1 = (f32[32,32,128]{2,1,0:T(8,128)S(1)}, f32[32,32,128]{2,1,0:T(8,128)}, u32[]{:S(2)}) copy-start(f32[32,32,128]{2,1,0:T(8,128)} %p.5) | copy-start | bytes 1572868
  7.8 14.4 %copy-start.2 = (f32[32,32,128]{2,1,0:T(8,128)S(1)}, f32[32,32,128]{2,1,0:T(8,128)}, u32[]{:S(2)}) copy-start(f32[32,32,128]{2,1,0:T(8,128)} %vx.5) | copy-start | bytes 1572868
  7.8 70.9 %all-to-all-start = ((f32[256,17,1,128]{3,2,1,0:T(1,128)}), f32[256,17,1,128]{3,2,1,0:T(1,128)S(1)}, u32[]{:S(2)}, u32[]{:S(2)}) async-start(f32[256,17,1,128]{3,2,1,0:T(1,128)} %bitcast.6), calls=%async_computation | async-start | bytes 4456448 | tf_op jit(solution)/shard_map/all_to_all | solution.py:306
  22.2 1.0 copy-start.3
  23.3 1.0 copy-start.5
  24.3 1.0 copy-start.7
  26.5 94.7 %collective-permute-start = (f32[5,8,32,128]{3,2,1,0:T(8,128)}, f32[5,8,32,128]{3,2,1,0:T(8,128)}, u32[]{:S(2)}, u32[]{:S(2)}) collective-permute-start(f32[5,8,32,128]{3,2,1,0:T(8,128)} %get-tuple-element.19), channel_id=1, source_target_pairs={{0,16},{16,32},{32,48},{48,64},{64,80},{80,96},{96,112},{112,128},... | collective-permute-start | bytes 1966088 | tf_op jit(solution)/shard_map/ppermute | solution.py:37
  33.0 88.2 %collective-permute-start.1 = (f32[5,8,32,128]{3,2,1,0:T(8,128)}, f32[5,8,32,128]{3,2,1,0:T(8,128)}, u32[]{:S(2)}, u32[]{:S(2)}) collective-permute-start(f32[5,8,32,128]{3,2,1,0:T(8,128)} %get-tuple-element.20), channel_id=1, source_target_pairs={{16,0},{32,16},{48,32},{64,48},{80,64},{96,80},{112,96},{128,112},... | collective-permute-start | bytes 1966088 | tf_op jit(solution)/shard_map/ppermute | solution.py:37
  78.8 42.5 %copy-start.4 = (f32[32,32,128]{2,1,0:T(8,128)S(1)}, f32[32,32,128]{2,1,0:T(8,128)}, u32[]{:S(2)}) copy-start(f32[32,32,128]{2,1,0:T(8,128)} %vy.5) | copy-start | bytes 1572868
  78.8 42.5 %copy-start.6 = (f32[32,32,128]{2,1,0:T(8,128)S(1)}, f32[32,32,128]{2,1,0:T(8,128)}, u32[]{:S(2)}) copy-start(f32[32,32,128]{2,1,0:T(8,128)} %vz.5) | copy-start | bytes 1572868
  78.8 42.5 %copy-start.8 = (s32[32,32,128]{2,1,0:T(8,128)S(1)}, s32[32,32,128]{2,1,0:T(8,128)}, u32[]{:S(2)}) copy-start(s32[32,32,128]{2,1,0:T(8,128)} %mat.5) | copy-start | bytes 1572868
  84.1 48.4 %collective-permute-start.4 = (f32[28,32,128]{2,1,0:T(8,128)S(1)}, f32[28,32,128]{2,1,0:T(8,128)S(1)}, u32[]{:S(2)}, u32[]{:S(2)}) collective-permute-start(f32[28,32,128]{2,1,0:T(8,128)S(1)} %get-tuple-element.30), channel_id=1, source_target_pairs={{0,16},{16,32},{32,48},{48,64},{64,80},{80,96},{96,112},{112,128},... | collective-permute-start | bytes 1376264 | tf_op jit(solution)/shard_map/ppermute | solution.py:37
  119.3 20.7 %collective-permute-start.5 = (f32[28,32,128]{2,1,0:T(8,128)S(1)}, f32[28,32,128]{2,1,0:T(8,128)S(1)}, u32[]{:S(2)}, u32[]{:S(2)}) collective-permute-start(f32[28,32,128]{2,1,0:T(8,128)S(1)} %get-tuple-element.31), channel_id=1, source_target_pairs={{16,0},{32,16},{48,32},{64,48},{80,64},{96,80},{112,96},{128,112},... | collective-permute-start | bytes 1376264 | tf_op jit(solution)/shard_map/ppermute | solution.py:37
  122.7 31.3 %collective-permute-start.2 = (f32[5,48,8,128]{3,2,1,0:T(8,128)S(1)}, f32[5,48,8,128]{3,2,1,0:T(8,128)S(1)}, u32[]{:S(2)}, u32[]{:S(2)}) collective-permute-start(f32[5,48,8,128]{3,2,1,0:T(8,128)S(1)} %get-tuple-element.21), channel_id=1, source_target_pairs={{0,1},{1,2},{2,3},{3,4},{4,5},{5,6},{6,7},{7,8},{8,9},{9,10},{10,1... | collective-permute-start | bytes 2949128 | tf_op jit(solution)/shard_map/ppermute | solution.py:37
  127.1 35.6 %collective-permute-start.3 = (f32[5,48,8,128]{3,2,1,0:T(8,128)S(1)}, f32[5,48,8,128]{3,2,1,0:T(8,128)S(1)}, u32[]{:S(2)}, u32[]{:S(2)}) collective-permute-start(f32[5,48,8,128]{3,2,1,0:T(8,128)S(1)} %get-tuple-element.22), channel_id=1, source_target_pairs={{1,0},{2,1},{3,2},{4,3},{5,4},{6,5},{7,6},{8,7},{9,8},{10,9},{11,1... | collective-permute-start | bytes 2949128 | tf_op jit(solution)/shard_map/ppermute | solution.py:37
  140.0 5.8 %copy-start.12 = (f32[4]{0:T(128)S(1)}, f32[4]{0:T(128)}, u32[]{:S(2)}) copy-start(f32[4]{0:T(128)} %param.16) | copy-start | bytes 52
  140.0 5.8 %copy-start.13 = (f32[4]{0:T(128)S(1)}, f32[4]{0:T(128)}, u32[]{:S(2)}) copy-start(f32[4]{0:T(128)} %param.15) | copy-start | bytes 52
  140.5 27.9 %collective-permute-start.6 = (f32[164,8,128]{2,1,0:T(8,128)S(1)}, f32[164,8,128]{2,1,0:T(8,128)S(1)}, u32[]{:S(2)}, u32[]{:S(2)}) collective-permute-start(f32[164,8,128]{2,1,0:T(8,128)S(1)} %get-tuple-element.32), channel_id=1, source_target_pairs={{0,1},{1,2},{2,3},{3,4},{4,5},{5,6},{6,7},{7,8},{8,9},{9,10},{10,1... | collective-permute-start | bytes 2015240 | tf_op jit(solution)/shard_map/ppermute | solution.py:37
  142.4 34.6 %collective-permute-start.7 = (f32[164,8,128]{2,1,0:T(8,128)S(1)}, f32[164,8,128]{2,1,0:T(8,128)S(1)}, u32[]{:S(2)}, u32[]{:S(2)}) collective-permute-start(f32[164,8,128]{2,1,0:T(8,128)S(1)} %get-tuple-element.33), channel_id=1, source_target_pairs={{1,0},{2,1},{3,2},{4,3},{5,4},{6,5},{7,6},{8,7},{9,8},{10,9},{11,1... | collective-permute-start | bytes 2015240 | tf_op jit(solution)/shard_map/ppermute | solution.py:37
where the time goes:
time: 192 us; the launch traced here: 191 us
  waiting for transfers between devices  82.5 us (43%)
  starting transfers between devices  71.5 us (37%)
  Pallas kernels  28.3 us (15%)
  local copies, waits for them, and re-layouts  7.1 us (4%)
    ppermute x8, starting transfers between devices, moved(): return lax.ppermute(block, axis, route)  57.2 us
    all_to_all x1, waiting for transfers between devices, program(): lax.all_to_all(outgoing.reshape(devices, block, 1, layers), ('gx', 'gy'),...  43.8 us
    ppermute x8, waiting for transfers between devices, moved(): return lax.ppermute(block, axis, route)  38.7 us
    all_to_all x1, starting transfers between devices, program(): lax.all_to_all(outgoing.reshape(devices, block, 1, layers), ('gx', 'gy'),...  14.4 us
    pallas_call x1, Pallas kernels, program(): call(step_kernel, [(wide, tall, layers)] * 4, [VMEM] * 11, 12, 32, [pltpu...  14.2 us
    unnamed x28, local copies, waits for them, and re-layouts  7.1 us
    pallas_call x1, Pallas kernels, program(): call(source_kernel, [(STEPS, wide, tall, layers)] + [(X_PLANES, tall, lay...  5.28 us
  transfers between devices with their start and end apart: 9, of which 7 were waited for; matrix products, arithmetic and copies ran while one was open for 0% of the time, Pallas kernels for 6%

commit v1 on v0

--- a/solution.py
+++ b/solution.py
@@ -20,7 +20,12 @@
 def call(kernel, outs, in_specs, micros, mib, scratch=()):
     return pl.pallas_call(
         kernel,
-        out_shape=[jax.ShapeDtypeStruct(shape, jnp.float32) for shape in outs],
+        out_shape=[
+            shape
+            if isinstance(shape, jax.ShapeDtypeStruct)
+            else jax.ShapeDtypeStruct(shape, jnp.float32)
+            for shape in outs
+        ],
         in_specs=in_specs,
         out_specs=[VMEM] * len(outs),
         scratch_shapes=list(scratch),
@@ -37,13 +42,20 @@
     return lax.ppermute(block, axis, route)
 
 
-def pack_kernel(p, vx, vy, vz, mat, first, last):
+def pack_kernel(p, vx, vy, vz, mat, first, last, ends, sems):
     wide = p.shape[0]
-    for a, ref in enumerate((p, vx, vy, vz)):
-        first[a] = ref[:DEPTH]
-        last[a] = ref[wide - DEPTH :]
-    first[4] = mat[:DEPTH].astype(jnp.float32) + 1.0
-    last[4] = mat[wide - DEPTH :].astype(jnp.float32) + 1.0
+    sides = (slice(0, DEPTH), slice(wide - DEPTH, wide))
+    copies = []
+    for a, ref in enumerate((p, vx, vy, vz, mat)):
+        for side, out in enumerate((first, last)):
+            target = out.at[a] if a < 4 else ends.at[side]
+            copies.append(pltpu.make_async_copy(ref.at[sides[side]], target, sems.at[a, side]))
+    for copy in copies:
+        copy.start()
+    for copy in copies:
+        copy.wait()
+    first[4] = ends[0].astype(jnp.float32) + 1.0
+    last[4] = ends[1].astype(jnp.float32) + 1.0
 
 
 def send_kernel(tile, rank, cell, vals, out):
@@ -143,76 +155,100 @@
     return total + jnp.dot(hot, parts[2], preferred_element_type=jnp.float32)
 
 
-def source_kernel(arrived, src, first, last, parts_ref):
+def place_columns(cells, parts_ref, src, base, at, chunk, tall):
+    hot = one_hot(cells, base * tall, chunk * tall)
+    layers = src.shape[-1]
+    for s in range(0, STEPS, 2):
+        span = slice(s * layers, (s + 2) * layers)
+        got = spread(hot, [parts_ref[n, :, span] for n in range(3)])
+        for m in range(2):
+            piece = got[:, m * layers : (m + 1) * layers]
+            src[s + m, pl.ds(at, chunk)] = piece.reshape(chunk, tall, layers)
+
+
+def source_ends_kernel(arrived, ends, first, last, cells_out, parts):
     block = 2 * STEPS + 1
     tiles = arrived.shape[0] // block
-    wide, tall, layers = src.shape[1:]
+    half, tall, layers = ends.shape[1:]
     named = jnp.transpose(arrived[pl.ds(2 * STEPS, tiles, stride=block), :])
     cells = jnp.concatenate([named[0:1], named[1:2]], axis=1)
+    cells_out[...] = jnp.broadcast_to(cells, cells_out.shape)
     for s in range(STEPS):
         for r in range(2):
             rows = pl.ds(r * STEPS + s, tiles, stride=block)
             for n, part in enumerate(thirds(arrived[rows, :])):
-                parts_ref[n, r * tiles : (r + 1) * tiles, s * layers : (s + 1) * layers] = part
-    chunk = 8
+                parts[n, r * tiles : (r + 1) * tiles, s * layers : (s + 1) * layers] = part
 
     def body(i, c):
-        hot = one_hot(cells, i * (chunk * tall), chunk * tall)
-        for s in range(0, STEPS, 2):
-            span = slice(s * layers, (s + 2) * layers)
-            got = spread(hot, [parts_ref[n, :, span] for n in range(3)])
-            for m in range(2):
-                piece = got[:, m * layers : (m + 1) * layers]
-                src[s + m, pl.ds(i * chunk, chunk)] = piece.reshape(chunk, tall, layers)
+        place_columns(cells, parts, ends, i * (2 * half - DEPTH), i * DEPTH, DEPTH, tall)
         return c
 
-    lax.fori_loop(0, wide // chunk, body, 0)
+    lax.fori_loop(0, 2, body, 0)
     for s in range(LAST):
         for d in range(1, LAST - s + 1):
-            first[X_START[s] + d - 1] = src[s, d - 1]
-            last[X_START[s] + d - 1] = src[s, wide - d]
-
-
-def y_start(q, wide):
-    return sum(wide + 2 * Y_REACH[t] for t in range(q))
-
-
-def source_edge_kernel(src, low, high, first, last):
-    wide, tall, layers = src.shape[1:]
-    row = lax.broadcasted_iota(jnp.int32, (8, layers), 0)
+            first[X_START[s] + d - 1] = ends[s, d - 1]
+            last[X_START[s] + d - 1] = ends[s, half - d]
+
+
+def source_middle_kernel(cells, parts, ends, middle, y_first, y_last):
+    half, tall, _ = middle.shape[1:]
+
+    def body(i, c):
+        at = i * DEPTH
+        place_columns(cells[:1], parts, middle, at + DEPTH, at, DEPTH, tall)
+        return c
+
+    lax.fori_loop(0, half // DEPTH, body, 0)
     for q in range(PAIRS):
-        near, far, reach = q, LAST - 1 - q, Y_REACH[q]
-        base = y_start(q, wide)
-
-        def pack(out, slot, a, b, is_first):
-            if b is None:
-                out[slot] = a
-            elif is_first:
-                out[slot] = jnp.where(row <= LAST - 1 - q, a, pltpu.roll(b, LAST - q, 0))
-            else:
-                out[slot] = jnp.where(row >= q + 1, a, pltpu.roll(b, q + 1, 0))
-
-        for out, at, is_first in ((first, 0, True), (last, tall - 8, False)):
+        for out, at, is_first in ((y_first, 0, True), (y_last, tall - 8, False)):
             rows = slice(at, at + 8)
-
-            def inner(i, c):
-                for u in range(4):
-                    x = i * 4 + u
-                    b = src[far, x, rows, :] if far != near else None
-                    pack(out, base + reach + x, src[near, x, rows, :], b, is_first)
-                return c
-
-            lax.fori_loop(0, wide // 4, inner, 0)
+            for ref, begin, count, to in (
+                (ends, 0, DEPTH, 0),
+                (middle, 0, half, DEPTH),
+                (ends, half - DEPTH, DEPTH, DEPTH + half),
+            ):
+
+                def inner(i, c):
+                    for u in range(4):
+                        x = i * 4 + u
+                        far = ref[LAST - 1 - q, begin + x, rows, :] if q < PAIRS - 1 else None
+                        out[q * 2 * half + to + x] = paired(
+                            q, ref[q, begin + x, rows, :], far, is_first
+                        )
+                    return c
+
+                lax.fori_loop(0, count // 4, inner, 0)
+
+
+def paired(q, near, far, is_first):
+    if far is None:
+        return near
+    row = lax.broadcasted_iota(jnp.int32, near.shape, 0)
+    if is_first:
+        return jnp.where(row <= LAST - 1 - q, near, pltpu.roll(far, LAST - q, 0))
+    return jnp.where(row >= q + 1, near, pltpu.roll(far, q + 1, 0))
+
+
+def corner_start(q):
+    return sum(2 * Y_REACH[t] for t in range(q))
+
+
+def source_corner_kernel(low, high, y_first, y_last):
+    tall = low.shape[1]
+    for q in range(PAIRS):
+        far, reach, base = LAST - 1 - q, Y_REACH[q], corner_start(q)
+        for out, at, is_first in ((y_first, 0, True), (y_last, tall - 8, False)):
+            rows = slice(at, at + 8)
             for d in range(1, reach + 1):
-                with_far = far != near and d <= q
-                for halo, slot in ((low, base + reach - d), (high, base + reach + wide + d - 1)):
-                    a = halo[X_START[near] + d - 1, rows, :]
-                    b = halo[X_START[far] + d - 1, rows, :] if with_far else None
-                    pack(out, slot, a, b, is_first)
+                both = far != q and d <= q
+                for halo, slot in ((low, base + reach - d), (high, base + reach + d - 1)):
+                    a = halo[X_START[q] + d - 1, rows, :]
+                    b = halo[X_START[far] + d - 1, rows, :] if both else None
+                    out[slot] = paired(q, a, b, is_first)
 
 
 def step_kernel(
-    p0, vx0, vy0, vz0, bb, ss, src, low, high, ylow, yhigh,
+    p0, vx0, vy0, vz0, bb, ss, ends, middle, low, high, ylow, yhigh, clow, chigh,
     p_out, vx_out, vy_out, vz_out, p, vx, vy, vz,
 ):
     wide, tall, layers = p_out.shape
@@ -225,9 +261,11 @@
         p_in, vx_in, vy_in, vz_in = (p0, vx0, vy0, vz0) if s == 0 else (p, vx, vy, vz)
         q = min(s, LAST - 1 - s)
 
-        def tiles(x):
-            slot = y_start(q, wide) + Y_REACH[q] + x
-            lo, hi = ylow[slot], yhigh[slot]
+        def tiles(x, corner=None):
+            lo, hi = (ylow[q * wide + x], yhigh[q * wide + x]) if corner is None else (
+                clow[corner_start(q) + Y_REACH[q] + corner],
+                chigh[corner_start(q) + Y_REACH[q] + corner],
+            )
             if s > LAST - 1 - s:
                 lo, hi = pltpu.roll(lo, LAST - q, 0), pltpu.roll(hi, q + 1, 0)
             return lo, hi
@@ -261,24 +299,28 @@
         before = p_in[begin - 1]
         carry = (p_cur, vx_in[begin - 1] - bb[begin - 1] * (p_cur - before))
         for d in range(depth, 0, -1):
-            lo, hi = tiles(-d) if d < depth else (blank, blank)
+            lo, hi = tiles(0, -d) if d < depth else (blank, blank)
             source = jnp.concatenate([lo, low[X_START[s] + d - 1], hi], axis=0)
             carry = row(DEPTH - d, carry, source)
 
-        def inner(n, carry):
-            for u in range(4):
-                i = n * 4 + u
-                if s == LAST:
-                    source = jnp.concatenate([blank, src[s, i], blank], axis=0)
-                else:
-                    lo, hi = tiles(i)
-                    source = jnp.concatenate([lo, src[s, i], hi], axis=0)
-                carry = row(i + DEPTH, carry, source)
-            return carry
-
-        carry = lax.fori_loop(0, wide // 4, inner, carry)
+        half = wide // 2
+        for ref, begin, count, to in (
+            (ends, 0, DEPTH, 0),
+            (middle, 0, half, DEPTH),
+            (ends, half - DEPTH, DEPTH, DEPTH + half),
+        ):
+
+            def inner(n, carry):
+                for u in range(4):
+                    i = n * 4 + u
+                    lo, hi = tiles(i + to) if s < LAST else (blank, blank)
+                    source = jnp.concatenate([lo, ref[s, begin + i], hi], axis=0)
+                    carry = row(i + to + DEPTH, carry, source)
+                return carry
+
+            carry = lax.fori_loop(0, count // 4, inner, carry)
         for d in range(1, depth + 1):
-            lo, hi = tiles(wide + d - 1) if d < depth else (blank, blank)
+            lo, hi = tiles(0, d - 1) if d < depth else (blank, blank)
             source = jnp.concatenate([lo, high[X_START[s] + d - 1], hi], axis=0)
             carry = row(DEPTH + wide + d - 1, carry, source)
 
@@ -297,7 +339,14 @@
     values = panel_vals.reshape(columns, STEPS, layers)
     state = (pressure, vel_x, vel_y, vel_z, material)
 
-    first, last = call(pack_kernel, [(5, DEPTH, tall, layers)] * 2, [VMEM] * 5, 1, 8)(*state)
+    first, last = call(
+        pack_kernel,
+        [(5, DEPTH, tall, layers)] * 2,
+        [pl.BlockSpec(memory_space=pltpu.HBM)] * 5,
+        1,
+        60,
+        [pltpu.VMEM((2, DEPTH, tall, layers), jnp.int32), pltpu.SemaphoreType.DMA((5, 2))],
+    )(*state)
     low, high = moved(last, "gx", 1), moved(first, "gx", -1)
     block = 2 * STEPS + 1
     (outgoing,) = call(
@@ -321,30 +370,40 @@
         b_table, s_table, *state, low, high, y_low, y_high
     )
 
-    src, s_first, s_last = call(
-        source_kernel,
-        [(STEPS, wide, tall, layers)] + [(X_PLANES, tall, layers)] * 2,
+    half = wide // 2
+    parts_shape = jax.ShapeDtypeStruct((3, 2 * devices, STEPS * layers), jnp.bfloat16)
+    ends, s_first, s_last, cells, parts = call(
+        source_ends_kernel,
+        [(STEPS, half, tall, layers)]
+        + [(X_PLANES, tall, layers)] * 2
+        + [(8, 2 * devices), parts_shape],
         [VMEM],
-        5,
+        3,
         26,
-        [pltpu.VMEM((3, 2 * devices, STEPS * layers), jnp.bfloat16)],
     )(arrived)
     s_low, s_high = moved(s_last, "gx", 1), moved(s_first, "gx", -1)
-    tiles = y_start(PAIRS, wide)
-    e_first, e_last = call(
-        source_edge_kernel, [(tiles, 8, layers)] * 2, [VMEM] * 3, 2, 12
-    )(src, s_low, s_high)
+    middle, e_first, e_last = call(
+        source_middle_kernel,
+        [(STEPS, half, tall, layers)] + [(PAIRS * wide, 8, layers)] * 2,
+        [VMEM] * 3,
+        3,
+        20,
+    )(cells, parts, ends)
     e_low, e_high = moved(e_last, "gy", 1), moved(e_first, "gy", -1)
+    c_first, c_last = call(
+        source_corner_kernel, [(corner_start(PAIRS), 8, layers)] * 2, [VMEM] * 2, 1, 8
+    )(s_low, s_high)
+    c_low, c_high = moved(c_last, "gy", 1), moved(c_first, "gy", -1)
 
     return tuple(
         call(
             step_kernel,
             [(wide, tall, layers)] * 4,
-            [VMEM] * 11,
+            [VMEM] * 14,
             12,
             32,
             [pltpu.VMEM(box, jnp.float32)] * 4,
-        )(*extended, src, s_low, s_high, e_low, e_high)
+        )(*extended, ends, middle, s_low, s_high, e_low, e_high, c_low, c_high)
     )
 
 

time: 192 us -> 187 us (0.974)
  the two profiles are of different devices: /device:TPU:87 before, /device:TPU:54 now
where the time goes in v1:
time: 187 us; the launch traced here: 184 us
  waiting for transfers between devices  90.7 us (49%)
  starting transfers between devices  55.3 us (30%)
  Pallas kernels  29.7 us (16%)
  local copies, waits for them, and re-layouts  6.35 us (3%)
    ppermute x10, waiting for transfers between devices, moved(): return lax.ppermute(block, axis, route)  90.7 us
    ppermute x10, starting transfers between devices, moved(): return lax.ppermute(block, axis, route)  41.1 us
    all_to_all x1, starting transfers between devices, program(): lax.all_to_all(outgoing.reshape(devices, block, 1, layers), ('gx', 'gy'),...  14.3 us
    pallas_call x1, Pallas kernels, program(): call(step_kernel, [(wide, tall, layers)] * 4, [VMEM] * 14, 12, 32, [pltpu...  13.8 us
    unnamed x36, local copies, waits for them, and re-layouts  6.35 us
  transfers between devices with their start and end apart: 11, of which 5 were waited for; matrix products, arithmetic and copies ran while one was open for 0% of the time, Pallas kernels for 7%

profile of v1, /device:TPU:54, one launch (start us, length us, event | category | flops | bytes accessed | tf_op | source)
XLA Modules:
  0.0 183.9 jit_solution(4380749085493899370)
XLA Ops:
  0.6 0.9 convert_reduce_fusion.rank
  1.6 0.0 copy-start.13
  1.6 1.2 copy-done.13
  2.8 0.7 copy-done.14
  3.5 0.7 copy-done.15
  4.2 2.3 %shard_map.132 = f32[4352,128]{1,0:T(8,128)S(1)} custom-call(s32[256]{0:T(256)S(1)} %bitcast.9, s32[256]{0:T(256)S(1)} %convert_reduce_fusion.rank, s32[256]{0:T(256)S(1)} %bitcast.10, f32[256,8,128]{2,1,0:T(8,128)S(1)} %bitcast.7), custom_call_target="tpu_custom_call" | custom-call | bytes 6000000 | tf_op jit(solution)/shard_map/pallas_call | solution.py:352
  6.5 1.4 copy-done
  7.9 14.3 %all-to-all-start = ((f32[256,17,1,128]{3,2,1,0:T(1,128)}), f32[256,17,1,128]{3,2,1,0:T(1,128)S(1)}, u32[]{:S(2)}, u32[]{:S(2)}) async-start(f32[256,17,1,128]{3,2,1,0:T(1,128)} %bitcast.6), calls=%async_computation | async-start | bytes 4456448 | tf_op jit(solution)/shard_map/all_to_all | solution.py:355
  22.1 0.0 copy-start.2
  22.2 2.6 %shard_map.129 = (f32[5,8,32,128]{3,2,1,0:T(8,128)}, f32[5,8,32,128]{3,2,1,0:T(8,128)}) custom-call(f32[32,32,128]{2,1,0:T(8,128)} %p.5, f32[32,32,128]{2,1,0:T(8,128)} %vx.5, f32[32,32,128]{2,1,0:T(8,128)} %vy.5, f32[32,32,128]{2,1,0:T(8,128)} %vz.5, s32[32,32,128]{2,1,0:T(8,128)} %mat.5), custom_call_target="tpu_custom_call" | custom-call | bytes 2000000 | tf_op jit(solution)/shard_map/pallas_call | solution.py:342
  24.8 2.0 %collective-permute-start = (f32[5,8,32,128]{3,2,1,0:T(8,128)}, f32[5,8,32,128]{3,2,1,0:T(8,128)S(1)}, u32[]{:S(2)}, u32[]{:S(2)}) collective-permute-start(f32[5,8,32,128]{3,2,1,0:T(8,128)} %get-tuple-element.24), channel_id=1, source_target_pairs={{0,16},{16,32},{32,48},{48,64},{64,80},{80,96},{96,112},{112,128},... | collective-permute-start | bytes 1966088 | tf_op jit(solution)/shard_map/ppermute | solution.py:42
  26.8 8.3 %collective-permute-start.1 = (f32[5,8,32,128]{3,2,1,0:T(8,128)}, f32[5,8,32,128]{3,2,1,0:T(8,128)S(1)}, u32[]{:S(2)}, u32[]{:S(2)}) collective-permute-start(f32[5,8,32,128]{3,2,1,0:T(8,128)} %get-tuple-element.25), channel_id=1, source_target_pairs={{16,0},{32,16},{48,32},{64,48},{80,64},{96,80},{112,96},{128,112},... | collective-permute-start | bytes 1966088 | tf_op jit(solution)/shard_map/ppermute | solution.py:42
  35.2 66.9 %collective-permute-done.low = f32[5,8,32,128]{3,2,1,0:T(8,128)S(1)} collective-permute-done((f32[5,8,32,128]{3,2,1,0:T(8,128)}, f32[5,8,32,128]{3,2,1,0:T(8,128)S(1)}, u32[]{:S(2)}, u32[]{:S(2)}) %collective-permute-start) | collective-permute-done | bytes 655392 | tf_op jit(solution)/shard_map/ppermute | solution.py:42
  102.1 1.3 copy-done.5
  103.3 1.0 copy-done.7
  104.4 1.5 shard_map.130
  105.9 2.4 %collective-permute-start.2 = (f32[5,48,8,128]{3,2,1,0:T(8,128)}, f32[5,48,8,128]{3,2,1,0:T(8,128)}, u32[]{:S(2)}, u32[]{:S(2)}) collective-permute-start(f32[5,48,8,128]{3,2,1,0:T(8,128)} %get-tuple-element.26), channel_id=1, source_target_pairs={{0,1},{1,2},{2,3},{3,4},{4,5},{5,6},{6,7},{7,8},{8,9},{9,10},{10,1... | collective-permute-start | bytes 2949128 | tf_op jit(solution)/shard_map/ppermute | solution.py:42
  108.3 3.5 %collective-permute-start.3 = (f32[5,48,8,128]{3,2,1,0:T(8,128)}, f32[5,48,8,128]{3,2,1,0:T(8,128)}, u32[]{:S(2)}, u32[]{:S(2)}) collective-permute-start(f32[5,48,8,128]{3,2,1,0:T(8,128)} %get-tuple-element.27), channel_id=1, source_target_pairs={{1,0},{2,1},{3,2},{4,3},{5,4},{6,5},{7,6},{8,7},{9,8},{10,9},{11,1... | collective-permute-start | bytes 2949128 | tf_op jit(solution)/shard_map/ppermute | solution.py:42
  111.8 3.3 %shard_map.133 = (f32[8,16,32,128]{3,2,1,0:T(8,128)S(1)}, f32[28,32,128]{2,1,0:T(8,128)S(1)}, f32[28,32,128]{2,1,0:T(8,128)S(1)}, f32[8,512]{1,0:T(8,128)S(1)}, bf16[3,512,1024]{2,1,0:T(8,128)(2,1)S(1)}) custom-call(f32[4352,128]{1,0:T(8,128)S(1)} %bitcast.5), custom_call_target="tpu_custom_call" | custom-call | bytes 6000000 | tf_op jit(solution)/shard_map/pallas_call | solution.py:375
  115.1 1.9 %collective-permute-start.4 = (f32[28,32,128]{2,1,0:T(8,128)S(1)}, f32[28,32,128]{2,1,0:T(8,128)S(1)}, u32[]{:S(2)}, u32[]{:S(2)}) collective-permute-start(f32[28,32,128]{2,1,0:T(8,128)S(1)} %get-tuple-element.38), channel_id=1, source_target_pairs={{0,16},{16,32},{32,48},{48,64},{64,80},{80,96},{96,112},{112,128},... | collective-permute-start | bytes 1376264 | tf_op jit(solution)/shard_map/ppermute | solution.py:42
  117.0 8.4 %collective-permute-start.5 = (f32[28,32,128]{2,1,0:T(8,128)S(1)}, f32[28,32,128]{2,1,0:T(8,128)S(1)}, u32[]{:S(2)}, u32[]{:S(2)}) collective-permute-start(f32[28,32,128]{2,1,0:T(8,128)S(1)} %get-tuple-element.39), channel_id=1, source_target_pairs={{16,0},{32,16},{48,32},{64,48},{80,64},{96,80},{112,96},{128,112},... | collective-permute-start | bytes 1376264 | tf_op jit(solution)/shard_map/ppermute | solution.py:42
  125.5 2.4 %shard_map.134 = (f32[8,16,32,128]{3,2,1,0:T(8,128)S(1)}, f32[128,8,128]{2,1,0:T(8,128)S(1)}, f32[128,8,128]{2,1,0:T(8,128)S(1)}) custom-call(f32[8,512]{1,0:T(8,128)S(1)} %get-tuple-element.35.cells, bf16[3,512,1024]{2,1,0:T(8,128)(2,1)S(1)} %get-tuple-element.36.parts, f32[8,16,32,128]{3,2,1,0:T(8,128)S(1)} %get-tuple-element.34.ends), custom_call_target="tpu_custom_call" | custom-call | bytes 6000000 | tf_op jit(solution)/shard_map/pallas_call | solution.py:385
  127.9 4.6 %collective-permute-start.6 = (f32[128,8,128]{2,1,0:T(8,128)S(1)}, f32[128,8,128]{2,1,0:T(8,128)S(1)}, u32[]{:S(2)}, u32[]{:S(2)}) collective-permute-start(f32[128,8,128]{2,1,0:T(8,128)S(1)} %get-tuple-element.40), channel_id=1, source_target_pairs={{0,1},{1,2},{2,3},{3,4},{4,5},{5,6},{6,7},{7,8},{8,9},{9,10},{10,1... | collective-permute-start | bytes 1572872 | tf_op jit(solution)/shard_map/ppermute | solution.py:42
  132.6 9.9 %collective-permute-done.4.low = f32[28,32,128]{2,1,0:T(8,128)S(1)} collective-permute-done((f32[28,32,128]{2,1,0:T(8,128)S(1)}, f32[28,32,128]{2,1,0:T(8,128)S(1)}, u32[]{:S(2)}, u32[]{:S(2)}) %collective-permute-start.4) | collective-permute-done | bytes 458784 | tf_op jit(solution)/shard_map/ppermute | solution.py:42
  142.5 1.9 %collective-permute-start.7 = (f32[128,8,128]{2,1,0:T(8,128)S(1)}, f32[128,8,128]{2,1,0:T(8,128)S(1)}, u32[]{:S(2)}, u32[]{:S(2)}) collective-permute-start(f32[128,8,128]{2,1,0:T(8,128)S(1)} %get-tuple-element.41), channel_id=1, source_target_pairs={{1,0},{2,1},{3,2},{4,3},{5,4},{6,5},{7,6},{8,7},{9,8},{10,9},{11,1... | collective-permute-start | bytes 1572872 | tf_op jit(solution)/shard_map/ppermute | solution.py:42
  144.4 6.0 %collective-permute-start.8 = (f32[36,8,128]{2,1,0:T(8,128)S(1)}, f32[36,8,128]{2,1,0:T(8,128)S(1)}, u32[]{:S(2)}, u32[]{:S(2)}) collective-permute-start(f32[36,8,128]{2,1,0:T(8,128)S(1)} %get-tuple-element.42), channel_id=1, source_target_pairs={{0,1},{1,2},{2,3},{3,4},{4,5},{5,6},{6,7},{7,8},{8,9},{9,10},{10,1... | collective-permute-start | bytes 442376 | tf_op jit(solution)/shard_map/ppermute | solution.py:42
  150.5 1.9 %collective-permute-start.9 = (f32[36,8,128]{2,1,0:T(8,128)S(1)}, f32[36,8,128]{2,1,0:T(8,128)S(1)}, u32[]{:S(2)}, u32[]{:S(2)}) collective-permute-start(f32[36,8,128]{2,1,0:T(8,128)S(1)} %get-tuple-element.43), channel_id=1, source_target_pairs={{1,0},{2,1},{3,2},{4,3},{5,4},{6,5},{7,6},{8,7},{9,8},{10,9},{11,1... | collective-permute-start | bytes 442376 | tf_op jit(solution)/shard_map/ppermute | solution.py:42
  152.5 3.7 %shard_map.131 = (f32[48,48,128]{2,1,0:T(8,128)S(1)}, f32[48,48,128]{2,1,0:T(8,128)S(1)}, f32[48,48,128]{2,1,0:T(8,128)S(1)}, f32[48,48,128]{2,1,0:T(8,128)S(1)}...) custom-call(f32[4]{0:T(128)S(1)} %get-tuple-element.45.btab, f32[4]{0:T(128)S(1)} %get-tuple-element.44.stab, ...), custom_call_target="tpu_custom_call" | custom-call | bytes 8000000 | tf_op jit(solution)/shard_map/pallas_call | solution.py:369
  156.2 5.4 %collective-permute-done.6.ylow = f32[128,8,128]{2,1,0:T(8,128)S(1)} collective-permute-done((f32[128,8,128]{2,1,0:T(8,128)S(1)}, f32[128,8,128]{2,1,0:T(8,128)S(1)}, u32[]{:S(2)}, u32[]{:S(2)}) %collective-permute-start.6) | collective-permute-done | bytes 524320 | tf_op jit(solution)/shard_map/ppermute | solution.py:42
  161.6 6.2 %collective-permute-done.7.yhigh = f32[128,8,128]{2,1,0:T(8,128)S(1)} collective-permute-done((f32[128,8,128]{2,1,0:T(8,128)S(1)}, f32[128,8,128]{2,1,0:T(8,128)S(1)}, u32[]{:S(2)}, u32[]{:S(2)}) %collective-permute-start.7) | collective-permute-done | bytes 524320 | tf_op jit(solution)/shard_map/ppermute | solution.py:42
  167.8 2.4 %collective-permute-done.9.chigh = f32[36,8,128]{2,1,0:T(8,128)S(1)} collective-permute-done((f32[36,8,128]{2,1,0:T(8,128)S(1)}, f32[36,8,128]{2,1,0:T(8,128)S(1)}, u32[]{:S(2)}, u32[]{:S(2)}) %collective-permute-start.9) | collective-permute-done | bytes 147488 | tf_op jit(solution)/shard_map/ppermute | solution.py:42
  170.2 13.8 %shard_map.136 = (f32[32,32,128]{2,1,0:T(8,128)}, f32[32,32,128]{2,1,0:T(8,128)}, f32[32,32,128]{2,1,0:T(8,128)}, f32[32,32,128]{2,1,0:T(8,128)}) custom-call(f32[48,48,128]{2,1,0:T(8,128)S(1)} %get-tuple-element.28.p0, f32[48,48,128]{2,1,0:T(8,128)S(1)} %get-tuple-element.29.vx0, f32[48,48,128]{2,1,0:T(8,128)S(1)} %get-tuple-element.30.vy0, ...), custom_call_target="tpu_custom_call" | custom-call | bytes 24000000 | tf_op jit(solution)/shard_map/pallas_call | solution.py:399
  (36 shorter events, 0.1 us)
Async XLA Ops:
  1.6 1.2 copy-start.13
  2.8 0.7 copy-start.14
  3.5 0.7 copy-start.15
  6.5 1.4 copy-start
  7.9 103.9 %all-to-all-start = ((f32[256,17,1,128]{3,2,1,0:T(1,128)}), f32[256,17,1,128]{3,2,1,0:T(1,128)S(1)}, u32[]{:S(2)}, u32[]{:S(2)}) async-start(f32[256,17,1,128]{3,2,1,0:T(1,128)} %bitcast.6), calls=%async_computation | async-start | bytes 4456448 | tf_op jit(solution)/shard_map/all_to_all | solution.py:355
  22.1 79.9 %copy-start.1 = (f32[32,32,128]{2,1,0:T(8,128)S(1)}, f32[32,32,128]{2,1,0:T(8,128)}, u32[]{:S(2)}) copy-start(f32[32,32,128]{2,1,0:T(8,128)} %p.5) | copy-start | bytes 1572868
  22.1 79.9 %copy-start.2 = (f32[32,32,128]{2,1,0:T(8,128)S(1)}, f32[32,32,128]{2,1,0:T(8,128)}, u32[]{:S(2)}) copy-start(f32[32,32,128]{2,1,0:T(8,128)} %vx.5) | copy-start | bytes 1572868
  22.1 79.9 %copy-start.3 = (f32[32,32,128]{2,1,0:T(8,128)S(1)}, f32[32,32,128]{2,1,0:T(8,128)}, u32[]{:S(2)}) copy-start(f32[32,32,128]{2,1,0:T(8,128)} %vy.5) | copy-start | bytes 1572868
  24.8 77.2 %collective-permute-start = (f32[5,8,32,128]{3,2,1,0:T(8,128)}, f32[5,8,32,128]{3,2,1,0:T(8,128)S(1)}, u32[]{:S(2)}, u32[]{:S(2)}) collective-permute-start(f32[5,8,32,128]{3,2,1,0:T(8,128)} %get-tuple-element.24), channel_id=1, source_target_pairs={{0,16},{16,32},{32,48},{48,64},{64,80},{80,96},{96,112},{112,128},... | collective-permute-start | bytes 1966088 | tf_op jit(solution)/shard_map/ppermute | solution.py:42
  26.8 75.2 %collective-permute-start.1 = (f32[5,8,32,128]{3,2,1,0:T(8,128)}, f32[5,8,32,128]{3,2,1,0:T(8,128)S(1)}, u32[]{:S(2)}, u32[]{:S(2)}) collective-permute-start(f32[5,8,32,128]{3,2,1,0:T(8,128)} %get-tuple-element.25), channel_id=1, source_target_pairs={{16,0},{32,16},{48,32},{64,48},{80,64},{96,80},{112,96},{128,112},... | collective-permute-start | bytes 1966088 | tf_op jit(solution)/shard_map/ppermute | solution.py:42
  102.0 3.9 %copy-start.9 = (f32[5,8,32,128]{3,2,1,0:T(8,128)}, f32[5,8,32,128]{3,2,1,0:T(8,128)S(1)}, u32[]{:S(2)}) copy-start(f32[5,8,32,128]{3,2,1,0:T(8,128)S(1)} %collective-permute-done.low) | copy-start | bytes 1966084
  102.1 1.3 copy-start.5
  103.3 1.0 copy-start.7
  104.4 1.5 copy-start.11
  105.9 44.6 %collective-permute-start.2 = (f32[5,48,8,128]{3,2,1,0:T(8,128)}, f32[5,48,8,128]{3,2,1,0:T(8,128)}, u32[]{:S(2)}, u32[]{:S(2)}) collective-permute-start(f32[5,48,8,128]{3,2,1,0:T(8,128)} %get-tuple-element.26), channel_id=1, source_target_pairs={{0,1},{1,2},{2,3},{3,4},{4,5},{5,6},{6,7},{7,8},{8,9},{9,10},{10,1... | collective-permute-start | bytes 2949128 | tf_op jit(solution)/shard_map/ppermute | solution.py:42
  108.3 44.2 %collective-permute-start.3 = (f32[5,48,8,128]{3,2,1,0:T(8,128)}, f32[5,48,8,128]{3,2,1,0:T(8,128)}, u32[]{:S(2)}, u32[]{:S(2)}) collective-permute-start(f32[5,48,8,128]{3,2,1,0:T(8,128)} %get-tuple-element.27), channel_id=1, source_target_pairs={{1,0},{2,1},{3,2},{4,3},{5,4},{6,5},{7,6},{8,7},{9,8},{10,9},{11,1... | collective-permute-start | bytes 2949128 | tf_op jit(solution)/shard_map/ppermute | solution.py:42
  115.1 27.4 %collective-permute-start.4 = (f32[28,32,128]{2,1,0:T(8,128)S(1)}, f32[28,32,128]{2,1,0:T(8,128)S(1)}, u32[]{:S(2)}, u32[]{:S(2)}) collective-permute-start(f32[28,32,128]{2,1,0:T(8,128)S(1)} %get-tuple-element.38), channel_id=1, source_target_pairs={{0,16},{16,32},{32,48},{48,64},{64,80},{80,96},{96,112},{112,128},... | collective-permute-start | bytes 1376264 | tf_op jit(solution)/shard_map/ppermute | solution.py:42
  117.0 27.4 %collective-permute-start.5 = (f32[28,32,128]{2,1,0:T(8,128)S(1)}, f32[28,32,128]{2,1,0:T(8,128)S(1)}, u32[]{:S(2)}, u32[]{:S(2)}) collective-permute-start(f32[28,32,128]{2,1,0:T(8,128)S(1)} %get-tuple-element.39), channel_id=1, source_target_pairs={{16,0},{32,16},{48,32},{64,48},{80,64},{96,80},{112,96},{128,112},... | collective-permute-start | bytes 1376264 | tf_op jit(solution)/shard_map/ppermute | solution.py:42
  125.4 27.0 %copy-start.16 = (f32[4]{0:T(128)S(1)}, f32[4]{0:T(128)}, u32[]{:S(2)}) copy-start(f32[4]{0:T(128)} %param.16) | copy-start | bytes 52
  125.5 27.0 %copy-start.17 = (f32[4]{0:T(128)S(1)}, f32[4]{0:T(128)}, u32[]{:S(2)}) copy-start(f32[4]{0:T(128)} %param.15) | copy-start | bytes 52
  125.5 27.0 %copy-start.6 = (f32[32,32,128]{2,1,0:T(8,128)S(1)}, f32[32,32,128]{2,1,0:T(8,128)}, u32[]{:S(2)}) copy-start(f32[32,32,128]{2,1,0:T(8,128)} %vz.5) | copy-start | bytes 1572868
  125.5 27.0 %copy-start.8 = (s32[32,32,128]{2,1,0:T(8,128)S(1)}, s32[32,32,128]{2,1,0:T(8,128)}, u32[]{:S(2)}) copy-start(s32[32,32,128]{2,1,0:T(8,128)} %mat.5) | copy-start | bytes 1572868
  125.5 27.0 %copy-start.10 = (f32[5,8,32,128]{3,2,1,0:T(8,128)S(1)}, f32[5,8,32,128]{3,2,1,0:T(8,128)}, u32[]{:S(2)}) copy-start(f32[5,8,32,128]{3,2,1,0:T(8,128)} %copy-done.9) | copy-start | bytes 1966084
  125.5 27.0 %copy-start.12 = (f32[5,8,32,128]{3,2,1,0:T(8,128)S(1)}, f32[5,8,32,128]{3,2,1,0:T(8,128)}, u32[]{:S(2)}) copy-start(f32[5,8,32,128]{3,2,1,0:T(8,128)} %copy-done.11) | copy-start | bytes 1966084
  127.9 24.6 %copy-start.4 = (f32[32,32,128]{2,1,0:T(8,128)S(1)}, f32[32,32,128]{2,1,0:T(8,128)}, u32[]{:S(2)}) copy-start(f32[32,32,128]{2,1,0:T(8,128)} %vy.5) | copy-start | bytes 1572868
  127.9 33.6 %collective-permute-start.6 = (f32[128,8,128]{2,1,0:T(8,128)S(1)}, f32[128,8,128]{2,1,0:T(8,128)S(1)}, u32[]{:S(2)}, u32[]{:S(2)}) collective-permute-start(f32[128,8,128]{2,1,0:T(8,128)S(1)} %get-tuple-element.40), channel_id=1, source_target_pairs={{0,1},{1,2},{2,3},{3,4},{4,5},{5,6},{6,7},{7,8},{8,9},{9,10},{10,1... | collective-permute-start | bytes 1572872 | tf_op jit(solution)/shard_map/ppermute | solution.py:42
  142.5 25.3 %collective-permute-start.7 = (f32[128,8,128]{2,1,0:T(8,128)S(1)}, f32[128,8,128]{2,1,0:T(8,128)S(1)}, u32[]{:S(2)}, u32[]{:S(2)}) collective-permute-start(f32[128,8,128]{2,1,0:T(8,128)S(1)} %get-tuple-element.41), channel_id=1, source_target_pairs={{1,0},{2,1},{3,2},{4,3},{5,4},{6,5},{7,6},{8,7},{9,8},{10,9},{11,1... | collective-permute-start | bytes 1572872 | tf_op jit(solution)/shard_map/ppermute | solution.py:42
  144.4 23.3 %collective-permute-start.8 = (f32[36,8,128]{2,1,0:T(8,128)S(1)}, f32[36,8,128]{2,1,0:T(8,128)S(1)}, u32[]{:S(2)}, u32[]{:S(2)}) collective-permute-start(f32[36,8,128]{2,1,0:T(8,128)S(1)} %get-tuple-element.42), channel_id=1, source_target_pairs={{0,1},{1,2},{2,3},{3,4},{4,5},{5,6},{6,7},{7,8},{8,9},{9,10},{10,1... | collective-permute-start | bytes 442376 | tf_op jit(solution)/shard_map/ppermute | solution.py:42
  150.5 19.7 %collective-permute-start.9 = (f32[36,8,128]{2,1,0:T(8,128)S(1)}, f32[36,8,128]{2,1,0:T(8,128)S(1)}, u32[]{:S(2)}, u32[]{:S(2)}) collective-permute-start(f32[36,8,128]{2,1,0:T(8,128)S(1)} %get-tuple-element.43), channel_id=1, source_target_pairs={{1,0},{2,1},{3,2},{4,3},{5,4},{6,5},{7,6},{8,7},{9,8},{10,9},{11,1... | collective-permute-start | bytes 442376 | tf_op jit(solution)/shard_map/ppermute | solution.py:42

commit v2 on v1

--- a/solution.py
+++ b/solution.py
@@ -1,3 +1,5 @@
+import functools
+
 import jax
 import jax.numpy as jnp
 from jax import lax
@@ -42,20 +44,28 @@
     return lax.ppermute(block, axis, route)
 
 
-def pack_kernel(p, vx, vy, vz, mat, first, last, ends, sems):
+def pack_kernel(p, vx, mat, vy, vz, first, last, first2, last2, ends, sems):
     wide = p.shape[0]
-    sides = (slice(0, DEPTH), slice(wide - DEPTH, wide))
     copies = []
-    for a, ref in enumerate((p, vx, vy, vz, mat)):
-        for side, out in enumerate((first, last)):
-            target = out.at[a] if a < 4 else ends.at[side]
-            copies.append(pltpu.make_async_copy(ref.at[sides[side]], target, sems.at[a, side]))
+    for a, ref in enumerate((p, vx, mat, vy, vz)):
+        late = a > 2
+        deep = DEPTH - 1 if late else DEPTH
+        for side, out in enumerate((first2, last2) if late else (first, last)):
+            begin = (wide - deep) * side
+            target = ends.at[side] if a == 2 else out.at[a - 3 if late else a]
+            copies.append(
+                pltpu.make_async_copy(ref.at[begin : begin + deep], target, sems.at[a, side])
+            )
     for copy in copies:
         copy.start()
     for copy in copies:
         copy.wait()
-    first[4] = ends[0].astype(jnp.float32) + 1.0
-    last[4] = ends[1].astype(jnp.float32) + 1.0
+    first[2] = ends[0].astype(jnp.float32) + 1.0
+    last[2] = ends[1].astype(jnp.float32) + 1.0
+
+
+def as_float(plane):
+    return plane if plane.dtype == jnp.float32 else plane.astype(jnp.float32) + 1.0
 
 
 def send_kernel(tile, rank, cell, vals, out):
@@ -86,55 +96,60 @@
     lax.fori_loop(0, vals.shape[0] // 8, place, 0)
 
 
-def edge_kernel(p, vx, vy, vz, mat, low, high, first, last):
-    wide, tall = p.shape[:2]
-    for a, ref in enumerate((p, vx, vy, vz, mat)):
+def edge_kernel(*refs):
+    pack_edges(refs[:-4], *refs[-4:], 0)
+
+
+def pack_edges(fields, low, high, first, last, base):
+    wide, tall = fields[0].shape[:2]
+    deep = low.shape[1]
+    for a, ref in enumerate(fields):
+        at = base + a * (wide + 2 * deep)
         for out, rows in ((first, slice(0, 8)), (last, slice(tall - 8, tall))):
-            out[a, :DEPTH] = low[a, :, rows, :]
-            inner = ref[:, rows, :]
-            if a == 4:
-                inner = inner.astype(jnp.float32) + 1.0
-            out[a, DEPTH : DEPTH + wide] = inner
-            out[a, DEPTH + wide :] = high[a, :, rows, :]
-
-
-def extend_kernel(btab, stab, p, vx, vy, vz, mat, low, high, ylow, yhigh, *outs):
-    wide, _ = p.shape[:2]
-
-    def put(x, a, parts):
-        full = jnp.concatenate(parts, axis=0)
-        if a < 4:
-            outs[a][x] = full
+            out[at : at + deep] = low[a, :, rows, :]
+            out[at + deep : at + deep + wide] = as_float(ref[:, rows, :])
+            out[at + deep + wide : at + wide + 2 * deep] = high[a, :, rows, :]
+
+
+def extend(count, base, *refs):
+    if len(refs) == 2 * count + 4:
+        tables, fields = (), refs[:count]
+        low, high, ylow, yhigh = refs[count : count + 4]
+        outs = refs[count + 4 :]
+    else:
+        tables, fields = refs[:2], refs[2 : 2 + count]
+        low, high, ylow, yhigh = refs[2 + count : 6 + count]
+        outs = refs[6 + count :]
+    wide = fields[0].shape[0]
+    deep = low.shape[1]
+    skip = DEPTH - deep
+
+    def put(x, a, middle):
+        at = base + a * (wide + 2 * deep) + x
+        full = jnp.concatenate([ylow[at], middle, yhigh[at]], axis=0)
+        if fields[a].dtype == jnp.float32:
+            outs[a][x + skip] = full
             return
+        btab, stab = tables
         b = jnp.zeros_like(full)
         s = jnp.zeros_like(full)
         for m in range(btab.shape[0]):
             b = jnp.where(full == float(m + 1), btab[m], b)
             s = jnp.where(full == float(m + 1), stab[m], s)
-        outs[4][x] = b
-        outs[5][x] = s
-
-    for a, ref in enumerate((p, vx, vy, vz, mat)):
-
-        def lower(i, c):
-            put(i, a, [ylow[a, i], low[a, i], yhigh[a, i]])
+        outs[a][x + skip] = b
+        outs[a + 1][x + skip] = s
+
+    for a, ref in enumerate(fields):
+        for i in range(deep):
+            put(i, a, low[a, i])
+            put(deep + wide + i, a, high[a, i])
+
+        def inner(i, c):
+            for u in range(2):
+                put(i * 2 + u + deep, a, as_float(ref[i * 2 + u]))
             return c
 
-        def inner(i, c):
-            mid = ref[i]
-            if a == 4:
-                mid = mid.astype(jnp.float32) + 1.0
-            put(i + DEPTH, a, [ylow[a, i + DEPTH], mid, yhigh[a, i + DEPTH]])
-            return c
-
-        def upper(i, c):
-            x = i + DEPTH + wide
-            put(x, a, [ylow[a, x], high[a, i], yhigh[a, x]])
-            return c
-
-        lax.fori_loop(0, DEPTH, lower, 0)
-        lax.fori_loop(0, wide, inner, 0)
-        lax.fori_loop(0, DEPTH, upper, 0)
+        lax.fori_loop(0, wide // 2, inner, 0)
 
 
 def thirds(v):
@@ -190,8 +205,9 @@
             last[X_START[s] + d - 1] = ends[s, half - d]
 
 
-def source_middle_kernel(cells, parts, ends, middle, y_first, y_last):
+def source_middle_kernel(cells, parts, ends, vy, vz, low, high, middle, y_first, y_last):
     half, tall, _ = middle.shape[1:]
+    pack_edges((vy, vz), low, high, y_first, y_last, PAIRS * 2 * half)
 
     def body(i, c):
         at = i * DEPTH
@@ -337,17 +353,18 @@
     earlier = (target[:, None] == target[None, :]) & (order[None, :] < order[:, None])
     rank = jnp.sum(earlier.astype(jnp.int32), axis=1)
     values = panel_vals.reshape(columns, STEPS, layers)
-    state = (pressure, vel_x, vel_y, vel_z, material)
-
-    first, last = call(
+    early, late = (pressure, vel_x, material), (vel_y, vel_z)
+    hbm = pl.BlockSpec(memory_space=pltpu.HBM)
+    first, last, first2, last2 = call(
         pack_kernel,
-        [(5, DEPTH, tall, layers)] * 2,
-        [pl.BlockSpec(memory_space=pltpu.HBM)] * 5,
+        [(3, DEPTH, tall, layers)] * 2 + [(2, DEPTH - 1, tall, layers)] * 2,
+        [hbm] * 5,
         1,
         60,
         [pltpu.VMEM((2, DEPTH, tall, layers), jnp.int32), pltpu.SemaphoreType.DMA((5, 2))],
-    )(*state)
+    )(*early, *late)
     low, high = moved(last, "gx", 1), moved(first, "gx", -1)
+    low2, high2 = moved(last2, "gx", 1), moved(first2, "gx", -1)
     block = 2 * STEPS + 1
     (outgoing,) = call(
         send_kernel, [(devices * block, layers)], [SMEM] * 3 + [VMEM], 3, 12
@@ -359,17 +376,18 @@
         concat_axis=0,
         tiled=True,
     ).reshape(devices * block, layers)
-    y_first, y_last = call(
-        edge_kernel, [(5, wide + 2 * DEPTH, 8, layers)] * 2, [VMEM] * 7, 2, 12
-    )(*state, low, high)
-    y_low, y_high = moved(y_last, "gy", 1), moved(y_first, "gy", -1)
     b_table = courant * (1.0 / density_table)
     s_table = courant * (density_table * speed_table * speed_table)
     box = (wide + 2 * DEPTH, tall + 2 * DEPTH, layers)
-    extended = call(extend_kernel, [box] * 6, [SMEM] * 2 + [VMEM] * 9, 4, 20)(
-        b_table, s_table, *state, low, high, y_low, y_high
-    )
-
+
+    tiles = len(early) * (wide + 2 * DEPTH)
+    y_first, y_last = call(
+        edge_kernel, [(tiles, 8, layers)] * 2, [VMEM] * 5, 2, 12
+    )(*early, low, high)
+    y_low, y_high = moved(y_last, "gy", 1), moved(y_first, "gy", -1)
+    p_box, vx_box, b_box, s_box = call(
+        functools.partial(extend, 3, 0), [box] * 4, [SMEM] * 2 + [VMEM] * 7, 3, 20
+    )(b_table, s_table, *early, low, high, y_low, y_high)
     half = wide // 2
     parts_shape = jax.ShapeDtypeStruct((3, 2 * devices, STEPS * layers), jnp.bfloat16)
     ends, s_first, s_last, cells, parts = call(
@@ -384,12 +402,17 @@
     s_low, s_high = moved(s_last, "gx", 1), moved(s_first, "gx", -1)
     middle, e_first, e_last = call(
         source_middle_kernel,
-        [(STEPS, half, tall, layers)] + [(PAIRS * wide, 8, layers)] * 2,
-        [VMEM] * 3,
+        [(STEPS, half, tall, layers)]
+        + [(PAIRS * wide + len(late) * (wide + 2 * DEPTH - 2), 8, layers)] * 2,
+        [VMEM] * 7,
         3,
-        20,
-    )(cells, parts, ends)
+        24,
+    )(cells, parts, ends, *late, low2, high2)
     e_low, e_high = moved(e_last, "gy", 1), moved(e_first, "gy", -1)
+    vy_box, vz_box = call(
+        functools.partial(extend, 2, PAIRS * wide), [box] * 2, [VMEM] * 6, 2, 20
+    )(*late, low2, high2, e_low, e_high)
+    boxes = (p_box, vx_box, vy_box, vz_box, b_box, s_box)
     c_first, c_last = call(
         source_corner_kernel, [(corner_start(PAIRS), 8, layers)] * 2, [VMEM] * 2, 1, 8
     )(s_low, s_high)
@@ -403,7 +426,7 @@
             12,
             32,
             [pltpu.VMEM(box, jnp.float32)] * 4,
-        )(*extended, ends, middle, s_low, s_high, e_low, e_high, c_low, c_high)
+        )(*boxes, ends, middle, s_low, s_high, e_low, e_high, c_low, c_high)
     )
 
 

time: 187 us -> 193 us (1.032)
  the two profiles are of different devices: /device:TPU:54 before, /device:TPU:225 now
where the time goes in v2:
time: 193 us; the launch traced here: 192 us
  starting transfers between devices  98.2 us (51%)
  waiting for transfers between devices  58.3 us (30%)
  Pallas kernels  29.8 us (15%)
  local copies, waits for them, and re-layouts  4.03 us (2%)
    ppermute x12, starting transfers between devices, moved(): return lax.ppermute(block, axis, route)  84.6 us
    all_to_all x1, waiting for transfers between devices, program(): lax.all_to_all(outgoing.reshape(devices, block, 1, layers), ('gx', 'gy'),...  32.2 us
    ppermute x12, waiting for transfers between devices, moved(): return lax.ppermute(block, axis, route)  26.1 us
    pallas_call x1, Pallas kernels, program(): call(step_kernel, [(wide, tall, layers)] * 4, [VMEM] * 14, 12, 32, [pltpu...  13.8 us
    all_to_all x1, starting transfers between devices, program(): lax.all_to_all(outgoing.reshape(devices, block, 1, layers), ('gx', 'gy'),...  13.6 us
    unnamed x22, local copies, waits for them, and re-layouts  4.03 us
  transfers between devices with their start and end apart: 13, of which 2 were waited for; matrix products, arithmetic and copies ran while one was open for 0% of the time, Pallas kernels for 7%

profile of v2, /device:TPU:225, one launch (start us, length us, event | category | flops | bytes accessed | tf_op | source)
XLA Modules:
  0.0 192.3 jit_solution(13429426963498818539)
XLA Ops:
  0.6 0.9 convert_reduce_fusion.rank
  1.6 0.0 copy-start.6
  1.6 1.2 copy-done.6
  2.8 0.7 copy-done.7
  3.5 0.7 copy-done.8
  4.2 2.3 %shard_map.132 = f32[4352,128]{1,0:T(8,128)S(1)} custom-call(s32[256]{0:T(256)S(1)} %bitcast.9, s32[256]{0:T(256)S(1)} %convert_reduce_fusion.rank, s32[256]{0:T(256)S(1)} %bitcast.10, f32[256,8,128]{2,1,0:T(8,128)S(1)} %bitcast.7), custom_call_target="tpu_custom_call" | custom-call | bytes 6000000 | tf_op jit(solution)/shard_map/pallas_call | solution.py:369
  6.5 1.4 copy-done
  7.9 13.6 %all-to-all-start = ((f32[256,17,1,128]{3,2,1,0:T(1,128)}), f32[256,17,1,128]{3,2,1,0:T(1,128)S(1)}, u32[]{:S(2)}, u32[]{:S(2)}) async-start(f32[256,17,1,128]{3,2,1,0:T(1,128)} %bitcast.6), calls=%async_computation | async-start | bytes 4456448 | tf_op jit(solution)/shard_map/all_to_all | solution.py:372
  21.4 2.5 %shard_map.129 = (f32[3,8,32,128]{3,2,1,0:T(8,128)}, f32[3,8,32,128]{3,2,1,0:T(8,128)}, f32[2,7,32,128]{3,2,1,0:T(8,128)}, f32[2,7,32,128]{3,2,1,0:T(8,128)}) custom-call(f32[32,32,128]{2,1,0:T(8,128)} %refs_2_.3, f32[32,32,128]{2,1,0:T(8,128)} %refs_3_.1, s32[32,32,128]{2,1,0:T(8,128)} %refs_4_.1, f32[32,32,128]{2,1,0:T(8,128)} %refs_0_.3, ...), custom_call_target="tpu_custom_call" | custom-call | bytes 2000000 | tf_op jit(solution)/shard_map/pallas_call | solution.py:358
  23.9 0.0 copy-start.1
  23.9 5.2 %collective-permute-start = (f32[3,8,32,128]{3,2,1,0:T(8,128)}, f32[3,8,32,128]{3,2,1,0:T(8,128)}, u32[]{:S(2)}, u32[]{:S(2)}) collective-permute-start(f32[3,8,32,128]{3,2,1,0:T(8,128)} %get-tuple-element.26), channel_id=1, source_target_pairs={{0,16},{16,32},{32,48},{48,64},{64,80},{80,96},{96,112},{112,128},... | collective-permute-start | bytes 1179656 | tf_op jit(solution)/shard_map/ppermute | solution.py:44
  29.1 1.9 collective-permute-start.1
  31.0 8.4 %collective-permute-start.4 = (f32[2,7,32,128]{3,2,1,0:T(8,128)}, f32[2,7,32,128]{3,2,1,0:T(8,128)S(1)}, u32[]{:S(2)}, u32[]{:S(2)}) collective-permute-start(f32[2,7,32,128]{3,2,1,0:T(8,128)} %get-tuple-element.32), channel_id=1, source_target_pairs={{0,16},{16,32},{32,48},{48,64},{64,80},{80,96},{96,112},{112,128},... | collective-permute-start | bytes 688136 | tf_op jit(solution)/shard_map/ppermute | solution.py:44
  39.5 1.9 collective-permute-start.5
  41.4 32.2 %all-to-all-done = f32[256,17,1,128]{3,2,1,0:T(1,128)S(1)} async-done(((f32[256,17,1,128]{3,2,1,0:T(1,128)}), f32[256,17,1,128]{3,2,1,0:T(1,128)S(1)}, u32[]{:S(2)}, u32[]{:S(2)}) %all-to-all-start) | async-done | bytes 2228256 | tf_op jit(solution)/shard_map/all_to_all | solution.py:372
  73.7 3.3 %shard_map.133 = (f32[8,16,32,128]{3,2,1,0:T(8,128)S(1)}, f32[28,32,128]{2,1,0:T(8,128)S(1)}, f32[28,32,128]{2,1,0:T(8,128)S(1)}, f32[8,512]{1,0:T(8,128)S(1)}, bf16[3,512,1024]{2,1,0:T(8,128)(2,1)S(1)}) custom-call(f32[4352,128]{1,0:T(8,128)S(1)} %bitcast.5), custom_call_target="tpu_custom_call" | custom-call | bytes 6000000 | tf_op jit(solution)/shard_map/pallas_call | solution.py:393
  77.0 29.2 %collective-permute-start.8 = (f32[28,32,128]{2,1,0:T(8,128)S(1)}, f32[28,32,128]{2,1,0:T(8,128)S(1)}, u32[]{:S(2)}, u32[]{:S(2)}) collective-permute-start(f32[28,32,128]{2,1,0:T(8,128)S(1)} %get-tuple-element.44), channel_id=1, source_target_pairs={{0,16},{16,32},{32,48},{48,64},{64,80},{80,96},{96,112},{112,128},... | collective-permute-start | bytes 1376264 | tf_op jit(solution)/shard_map/ppermute | solution.py:44
  106.3 0.0 copy-start.4
  106.3 0.0 copy-start.5
  106.3 3.5 %shard_map.134 = (f32[8,16,32,128]{3,2,1,0:T(8,128)S(1)}, f32[220,8,128]{2,1,0:T(8,128)S(1)}, f32[220,8,128]{2,1,0:T(8,128)S(1)}) custom-call(f32[8,512]{1,0:T(8,128)S(1)} %get-tuple-element.34.cells, bf16[3,512,1024]{2,1,0:T(8,128)(2,1)S(1)} %get-tuple-element.35.parts, f32[8,16,32,128]{3,2,1,0:T(8,128)S(1)} %get-tuple-element.36.ends, ...), custom_call_target="tpu_custom_call" | custom-call | bytes 6000000 | tf_op jit(solution)/shard_map/pallas_call | solution.py:403
  109.8 3.6 %collective-permute-start.6 = (f32[220,8,128]{2,1,0:T(8,128)S(1)}, f32[220,8,128]{2,1,0:T(8,128)S(1)}, u32[]{:S(2)}, u32[]{:S(2)}) collective-permute-start(f32[220,8,128]{2,1,0:T(8,128)S(1)} %get-tuple-element.37), channel_id=1, source_target_pairs={{0,1},{1,2},{2,3},{3,4},{4,5},{5,6},{6,7},{7,8},{8,9},{9,10},{10,1... | collective-permute-start | bytes 2703368 | tf_op jit(solution)/shard_map/ppermute | solution.py:44
  113.4 3.8 %collective-permute-start.7 = (f32[220,8,128]{2,1,0:T(8,128)S(1)}, f32[220,8,128]{2,1,0:T(8,128)S(1)}, u32[]{:S(2)}, u32[]{:S(2)}) collective-permute-start(f32[220,8,128]{2,1,0:T(8,128)S(1)} %get-tuple-element.38), channel_id=1, source_target_pairs={{1,0},{2,1},{3,2},{4,3},{5,4},{6,5},{7,6},{8,7},{9,8},{10,9},{11,1... | collective-permute-start | bytes 2703368 | tf_op jit(solution)/shard_map/ppermute | solution.py:44
  117.3 1.2 shard_map.130
  118.5 1.9 collective-permute-start.2
  120.4 3.1 %collective-permute-start.9 = (f32[28,32,128]{2,1,0:T(8,128)S(1)}, f32[28,32,128]{2,1,0:T(8,128)S(1)}, u32[]{:S(2)}, u32[]{:S(2)}) collective-permute-start(f32[28,32,128]{2,1,0:T(8,128)S(1)} %get-tuple-element.45), channel_id=1, source_target_pairs={{16,0},{32,16},{48,32},{64,48},{80,64},{96,80},{112,96},{128,112},... | collective-permute-start | bytes 1376264 | tf_op jit(solution)/shard_map/ppermute | solution.py:44
  123.6 5.8 %collective-permute-start.3 = (f32[144,8,128]{2,1,0:T(8,128)S(1)}, f32[144,8,128]{2,1,0:T(8,128)S(1)}, u32[]{:S(2)}, u32[]{:S(2)}) collective-permute-start(f32[144,8,128]{2,1,0:T(8,128)S(1)} %get-tuple-element.29), channel_id=1, source_target_pairs={{1,0},{2,1},{3,2},{4,3},{5,4},{6,5},{7,6},{8,7},{9,8},{10,9},{11,1... | collective-permute-start | bytes 1769480 | tf_op jit(solution)/shard_map/ppermute | solution.py:44
  129.4 26.1 %collective-permute-done.9.high = f32[28,32,128]{2,1,0:T(8,128)S(1)} collective-permute-done((f32[28,32,128]{2,1,0:T(8,128)S(1)}, f32[28,32,128]{2,1,0:T(8,128)S(1)}, u32[]{:S(2)}, u32[]{:S(2)}) %collective-permute-start.9) | collective-permute-done | bytes 458784 | tf_op jit(solution)/shard_map/ppermute | solution.py:44
  155.4 1.9 collective-permute-start.10
  157.4 17.8 %collective-permute-start.11 = (f32[36,8,128]{2,1,0:T(8,128)S(1)}, f32[36,8,128]{2,1,0:T(8,128)S(1)}, u32[]{:S(2)}, u32[]{:S(2)}) collective-permute-start(f32[36,8,128]{2,1,0:T(8,128)S(1)} %get-tuple-element.47), channel_id=1, source_target_pairs={{1,0},{2,1},{3,2},{4,3},{5,4},{6,5},{7,6},{8,7},{9,8},{10,9},{11,1... | collective-permute-start | bytes 442376 | tf_op jit(solution)/shard_map/ppermute | solution.py:44
  175.2 2.0 %shard_map.131 = (f32[48,48,128]{2,1,0:T(8,128)S(1)}, f32[48,48,128]{2,1,0:T(8,128)S(1)}, f32[48,48,128]{2,1,0:T(8,128)S(1)}, f32[48,48,128]{2,1,0:T(8,128)S(1)}) custom-call(f32[4]{0:T(128)S(1)} %get-tuple-element.49.refs_0_, f32[4]{0:T(128)S(1)} %get-tuple-element.48.refs_1_, f32[32,32,128]{2,1,0:T(8,128)S(1)} %copy-done.3, f32[32,32,128]{2,1,0:T(8,128)S(1)} %copy-done.4, ...), custom_call_target="tpu_custom_call" | custom-call | bytes 6000000 | tf_op jit(solution)/shard_map/pallas_call | solution.py:388
  177.3 1.2 shard_map.135
  178.5 13.8 %shard_map.137 = (f32[32,32,128]{2,1,0:T(8,128)}, f32[32,32,128]{2,1,0:T(8,128)}, f32[32,32,128]{2,1,0:T(8,128)}, f32[32,32,128]{2,1,0:T(8,128)}) custom-call(f32[48,48,128]{2,1,0:T(8,128)S(1)} %get-tuple-element.30.p0, f32[48,48,128]{2,1,0:T(8,128)S(1)} %get-tuple-element.31.vx0, f32[48,48,128]{2,1,0:T(8,128)S(1)} %get-tuple-element.39.vy0, ...), custom_call_target="tpu_custom_call" | custom-call | bytes 24000000 | tf_op jit(solution)/shard_map/pallas_call | solution.py:422
  (27 shorter events, 0.1 us)
Async XLA Ops:
  1.6 1.2 copy-start.6
  2.8 0.7 copy-start.7
  3.5 0.7 copy-start.8
  6.5 1.4 copy-start
  7.9 65.8 %all-to-all-start = ((f32[256,17,1,128]{3,2,1,0:T(1,128)}), f32[256,17,1,128]{3,2,1,0:T(1,128)S(1)}, u32[]{:S(2)}, u32[]{:S(2)}) async-start(f32[256,17,1,128]{3,2,1,0:T(1,128)} %bitcast.6), calls=%async_computation | async-start | bytes 4456448 | tf_op jit(solution)/shard_map/all_to_all | solution.py:372
  23.9 82.3 %copy-start.1 = (f32[32,32,128]{2,1,0:T(8,128)S(1)}, f32[32,32,128]{2,1,0:T(8,128)}, u32[]{:S(2)}) copy-start(f32[32,32,128]{2,1,0:T(8,128)} %refs_0_.3) | copy-start | bytes 1572868
  23.9 82.3 %copy-start.2 = (f32[32,32,128]{2,1,0:T(8,128)S(1)}, f32[32,32,128]{2,1,0:T(8,128)}, u32[]{:S(2)}) copy-start(f32[32,32,128]{2,1,0:T(8,128)} %refs_1_.3) | copy-start | bytes 1572868
  23.9 93.3 %collective-permute-start = (f32[3,8,32,128]{3,2,1,0:T(8,128)}, f32[3,8,32,128]{3,2,1,0:T(8,128)}, u32[]{:S(2)}, u32[]{:S(2)}) collective-permute-start(f32[3,8,32,128]{3,2,1,0:T(8,128)} %get-tuple-element.26), channel_id=1, source_target_pairs={{0,16},{16,32},{32,48},{48,64},{64,80},{80,96},{96,112},{112,128},... | collective-permute-start | bytes 1179656 | tf_op jit(solution)/shard_map/ppermute | solution.py:44
  29.1 88.1 %collective-permute-start.1 = (f32[3,8,32,128]{3,2,1,0:T(8,128)}, f32[3,8,32,128]{3,2,1,0:T(8,128)}, u32[]{:S(2)}, u32[]{:S(2)}) collective-permute-start(f32[3,8,32,128]{3,2,1,0:T(8,128)} %get-tuple-element.27), channel_id=1, source_target_pairs={{16,0},{32,16},{48,32},{64,48},{80,64},{96,80},{112,96},{128,112},... | collective-permute-start | bytes 1179656 | tf_op jit(solution)/shard_map/ppermute | solution.py:44
  31.0 75.2 %collective-permute-start.4 = (f32[2,7,32,128]{3,2,1,0:T(8,128)}, f32[2,7,32,128]{3,2,1,0:T(8,128)S(1)}, u32[]{:S(2)}, u32[]{:S(2)}) collective-permute-start(f32[2,7,32,128]{3,2,1,0:T(8,128)} %get-tuple-element.32), channel_id=1, source_target_pairs={{0,16},{16,32},{32,48},{48,64},{64,80},{80,96},{96,112},{112,128},... | collective-permute-start | bytes 688136 | tf_op jit(solution)/shard_map/ppermute | solution.py:44
  39.5 66.7 %collective-permute-start.5 = (f32[2,7,32,128]{3,2,1,0:T(8,128)}, f32[2,7,32,128]{3,2,1,0:T(8,128)}, u32[]{:S(2)}, u32[]{:S(2)}) collective-permute-start(f32[2,7,32,128]{3,2,1,0:T(8,128)} %get-tuple-element.33), channel_id=1, source_target_pairs={{16,0},{32,16},{48,32},{64,48},{80,64},{96,80},{112,96},{128,112},... | collective-permute-start | bytes 688136 | tf_op jit(solution)/shard_map/ppermute | solution.py:44
  77.0 46.6 %collective-permute-start.8 = (f32[28,32,128]{2,1,0:T(8,128)S(1)}, f32[28,32,128]{2,1,0:T(8,128)S(1)}, u32[]{:S(2)}, u32[]{:S(2)}) collective-permute-start(f32[28,32,128]{2,1,0:T(8,128)S(1)} %get-tuple-element.44), channel_id=1, source_target_pairs={{0,16},{16,32},{32,48},{48,64},{64,80},{80,96},{96,112},{112,128},... | collective-permute-start | bytes 1376264 | tf_op jit(solution)/shard_map/ppermute | solution.py:44
  106.3 11.0 %copy-start.3 = (f32[32,32,128]{2,1,0:T(8,128)S(1)}, f32[32,32,128]{2,1,0:T(8,128)}, u32[]{:S(2)}) copy-start(f32[32,32,128]{2,1,0:T(8,128)} %refs_2_.3) | copy-start | bytes 1572868
  106.3 11.0 %copy-start.4 = (f32[32,32,128]{2,1,0:T(8,128)S(1)}, f32[32,32,128]{2,1,0:T(8,128)}, u32[]{:S(2)}) copy-start(f32[32,32,128]{2,1,0:T(8,128)} %refs_3_.1) | copy-start | bytes 1572868
  106.3 11.0 %copy-start.5 = (s32[32,32,128]{2,1,0:T(8,128)S(1)}, s32[32,32,128]{2,1,0:T(8,128)}, u32[]{:S(2)}) copy-start(s32[32,32,128]{2,1,0:T(8,128)} %refs_4_.1) | copy-start | bytes 1572868
  109.8 67.4 %collective-permute-start.6 = (f32[220,8,128]{2,1,0:T(8,128)S(1)}, f32[220,8,128]{2,1,0:T(8,128)S(1)}, u32[]{:S(2)}, u32[]{:S(2)}) collective-permute-start(f32[220,8,128]{2,1,0:T(8,128)S(1)} %get-tuple-element.37), channel_id=1, source_target_pairs={{0,1},{1,2},{2,3},{3,4},{4,5},{5,6},{6,7},{7,8},{8,9},{9,10},{10,1... | collective-permute-start | bytes 2703368 | tf_op jit(solution)/shard_map/ppermute | solution.py:44
  113.4 61.8 %copy-start.9 = (f32[4]{0:T(128)S(1)}, f32[4]{0:T(128)}, u32[]{:S(2)}) copy-start(f32[4]{0:T(128)} %param.16) | copy-start | bytes 52
  113.4 61.8 %copy-start.10 = (f32[4]{0:T(128)S(1)}, f32[4]{0:T(128)}, u32[]{:S(2)}) copy-start(f32[4]{0:T(128)} %param.15) | copy-start | bytes 52
  113.4 63.9 %collective-permute-start.7 = (f32[220,8,128]{2,1,0:T(8,128)S(1)}, f32[220,8,128]{2,1,0:T(8,128)S(1)}, u32[]{:S(2)}, u32[]{:S(2)}) collective-permute-start(f32[220,8,128]{2,1,0:T(8,128)S(1)} %get-tuple-element.38), channel_id=1, source_target_pairs={{1,0},{2,1},{3,2},{4,3},{5,4},{6,5},{7,6},{8,7},{9,8},{10,9},{11,1... | collective-permute-start | bytes 2703368 | tf_op jit(solution)/shard_map/ppermute | solution.py:44
  118.5 38.9 %collective-permute-start.2 = (f32[144,8,128]{2,1,0:T(8,128)S(1)}, f32[144,8,128]{2,1,0:T(8,128)S(1)}, u32[]{:S(2)}, u32[]{:S(2)}) collective-permute-start(f32[144,8,128]{2,1,0:T(8,128)S(1)} %get-tuple-element.28), channel_id=1, source_target_pairs={{0,1},{1,2},{2,3},{3,4},{4,5},{5,6},{6,7},{7,8},{8,9},{9,10},{10,1... | collective-permute-start | bytes 1769480 | tf_op jit(solution)/shard_map/ppermute | solution.py:44
  120.4 35.0 %collective-permute-start.9 = (f32[28,32,128]{2,1,0:T(8,128)S(1)}, f32[28,32,128]{2,1,0:T(8,128)S(1)}, u32[]{:S(2)}, u32[]{:S(2)}) collective-permute-start(f32[28,32,128]{2,1,0:T(8,128)S(1)} %get-tuple-element.45), channel_id=1, source_target_pairs={{16,0},{32,16},{48,32},{64,48},{80,64},{96,80},{112,96},{128,112},... | collective-permute-start | bytes 1376264 | tf_op jit(solution)/shard_map/ppermute | solution.py:44
  123.6 51.6 %collective-permute-start.3 = (f32[144,8,128]{2,1,0:T(8,128)S(1)}, f32[144,8,128]{2,1,0:T(8,128)S(1)}, u32[]{:S(2)}, u32[]{:S(2)}) collective-permute-start(f32[144,8,128]{2,1,0:T(8,128)S(1)} %get-tuple-element.29), channel_id=1, source_target_pairs={{1,0},{2,1},{3,2},{4,3},{5,4},{6,5},{7,6},{8,7},{9,8},{10,9},{11,1... | collective-permute-start | bytes 1769480 | tf_op jit(solution)/shard_map/ppermute | solution.py:44
  155.4 23.0 %collective-permute-start.10 = (f32[36,8,128]{2,1,0:T(8,128)S(1)}, f32[36,8,128]{2,1,0:T(8,128)S(1)}, u32[]{:S(2)}, u32[]{:S(2)}) collective-permute-start(f32[36,8,128]{2,1,0:T(8,128)S(1)} %get-tuple-element.46), channel_id=1, source_target_pairs={{0,1},{1,2},{2,3},{3,4},{4,5},{5,6},{6,7},{7,8},{8,9},{9,10},{10,1... | collective-permute-start | bytes 442376 | tf_op jit(solution)/shard_map/ppermute | solution.py:44
  157.4 21.1 %collective-permute-start.11 = (f32[36,8,128]{2,1,0:T(8,128)S(1)}, f32[36,8,128]{2,1,0:T(8,128)S(1)}, u32[]{:S(2)}, u32[]{:S(2)}) collective-permute-start(f32[36,8,128]{2,1,0:T(8,128)S(1)} %get-tuple-element.47), channel_id=1, source_target_pairs={{1,0},{2,1},{3,2},{4,3},{5,4},{6,5},{7,6},{8,7},{9,8},{10,9},{11,1... | collective-permute-start | bytes 442376 | tf_op jit(solution)/shard_map/ppermute | solution.py:44

commit v3 on v2

--- a/solution.py
+++ b/solution.py
@@ -19,7 +19,7 @@
 SMEM = pl.BlockSpec(memory_space=pltpu.SMEM)
 
 
-def call(kernel, outs, in_specs, micros, mib, scratch=()):
+def call(kernel, outs, in_specs, micros, mib, scratch=(), out_spec=VMEM):
     return pl.pallas_call(
         kernel,
         out_shape=[
@@ -29,7 +29,7 @@
             for shape in outs
         ],
         in_specs=in_specs,
-        out_specs=[VMEM] * len(outs),
+        out_specs=[out_spec] * len(outs),
         scratch_shapes=list(scratch),
         compiler_params=pltpu.CompilerParams(vmem_limit_bytes=mib << 20),
         cost_estimate=pl.CostEstimate(
@@ -96,8 +96,14 @@
     lax.fori_loop(0, vals.shape[0] // 8, place, 0)
 
 
-def edge_kernel(*refs):
-    pack_edges(refs[:-4], *refs[-4:], 0)
+def edge_kernel(p, vx, mat, vy, vz, low, high, first, last):
+    pack_edges((p, vx, mat), low, high, first, last, 0)
+    wide, tall = vy.shape[:2]
+    begin = 3 * (wide + 2 * DEPTH)
+    for a, ref in enumerate((vy, vz)):
+        rows = slice(begin + a * wide, begin + (a + 1) * wide)
+        first[rows] = ref[:, :8, :]
+        last[rows] = ref[:, tall - 8 :, :]
 
 
 def pack_edges(fields, low, high, first, last, base):
@@ -152,6 +158,28 @@
         lax.fori_loop(0, wide // 2, inner, 0)
 
 
+def extend_late_kernel(vy, vz, low, high, ylow, yhigh, elow, ehigh, *outs):
+    wide = vy.shape[0]
+    deep = low.shape[1]
+    for a, (ref, out) in enumerate(zip((vy, vz), outs)):
+        main = 3 * (wide + 2 * DEPTH) + a * wide
+        side = PAIRS * wide + 2 * a * deep
+        for i in range(deep):
+            k = side + i
+            out[DEPTH - deep + i] = jnp.concatenate([elow[k], low[a, i], ehigh[k]], axis=0)
+            k = side + deep + i
+            out[DEPTH + wide + i] = jnp.concatenate([elow[k], high[a, i], ehigh[k]], axis=0)
+
+        def inner(n, c):
+            for u in range(2):
+                i = n * 2 + u
+                parts = [ylow[main + i], ref[i], yhigh[main + i]]
+                out[i + DEPTH] = jnp.concatenate(parts, axis=0)
+            return c
+
+        lax.fori_loop(0, wide // 2, inner, 0)
+
+
 def thirds(v):
     hi = v.astype(jnp.bfloat16)
     rest = v - hi.astype(jnp.float32)
@@ -205,9 +233,14 @@
             last[X_START[s] + d - 1] = ends[s, half - d]
 
 
-def source_middle_kernel(cells, parts, ends, vy, vz, low, high, middle, y_first, y_last):
+def source_middle_kernel(cells, parts, ends, low, high, middle, y_first, y_last):
     half, tall, _ = middle.shape[1:]
-    pack_edges((vy, vz), low, high, y_first, y_last, PAIRS * 2 * half)
+    deep = low.shape[1]
+    for a in range(low.shape[0]):
+        for n, halo in enumerate((low, high)):
+            begin = PAIRS * 2 * half + (2 * a + n) * deep
+            y_first[begin : begin + deep] = halo[a, :, :8, :]
+            y_last[begin : begin + deep] = halo[a, :, tall - 8 :, :]
 
     def body(i, c):
         at = i * DEPTH
@@ -265,9 +298,10 @@
 
 def step_kernel(
     p0, vx0, vy0, vz0, bb, ss, ends, middle, low, high, ylow, yhigh, clow, chigh,
-    p_out, vx_out, vy_out, vz_out, p, vx, vy, vz,
+    p_out, vx_out, vy_out, vz_out, p, vx, vy, vz, done, sems,
 ):
     wide, tall, layers = p_out.shape
+    copies = []
     full = tall + 2 * DEPTH
     lane = lax.broadcasted_iota(jnp.int32, (full, layers), 1)
     blank = jnp.zeros((8, layers), jnp.float32)
@@ -299,10 +333,8 @@
             p_new = p_cur + ss[i] * (source - div)
             if s == LAST:
                 keep = slice(DEPTH, DEPTH + tall)
-                p_out[i - DEPTH] = p_new[keep]
-                vx_out[i - DEPTH] = vx_new[keep]
-                vy_out[i - DEPTH] = vy_new[keep]
-                vz_out[i - DEPTH] = vz_new[keep]
+                for a, new in enumerate((p_new, vx_new, vy_new, vz_new)):
+                    done[a, i - DEPTH] = new[keep]
             else:
                 p[i] = p_new
                 vx[i] = vx_new
@@ -327,18 +359,26 @@
         ):
 
             def inner(n, carry):
-                for u in range(4):
-                    i = n * 4 + u
+                for u in range(8):
+                    i = n * 8 + u
                     lo, hi = tiles(i + to) if s < LAST else (blank, blank)
                     source = jnp.concatenate([lo, ref[s, begin + i], hi], axis=0)
                     carry = row(i + to + DEPTH, carry, source)
                 return carry
 
-            carry = lax.fori_loop(0, count // 4, inner, carry)
+            carry = lax.fori_loop(0, count // 8, inner, carry)
+            if s == LAST:
+                rows = pl.ds(to, count)
+                for a, out in enumerate((p_out, vx_out, vy_out, vz_out)):
+                    sem = sems.at[a, len(copies) // 4]
+                    copies.append(pltpu.make_async_copy(done.at[a, rows], out.at[rows], sem))
+                    copies[-1].start()
         for d in range(1, depth + 1):
             lo, hi = tiles(0, d - 1) if d < depth else (blank, blank)
             source = jnp.concatenate([lo, high[X_START[s] + d - 1], hi], axis=0)
             carry = row(DEPTH + wide + d - 1, carry, source)
+    for copy in copies:
+        copy.wait()
 
 
 def program(
@@ -380,10 +420,10 @@
     s_table = courant * (density_table * speed_table * speed_table)
     box = (wide + 2 * DEPTH, tall + 2 * DEPTH, layers)
 
-    tiles = len(early) * (wide + 2 * DEPTH)
+    tiles = 3 * (wide + 2 * DEPTH) + 2 * wide
     y_first, y_last = call(
-        edge_kernel, [(tiles, 8, layers)] * 2, [VMEM] * 5, 2, 12
-    )(*early, low, high)
+        edge_kernel, [(tiles, 8, layers)] * 2, [VMEM] * 7, 2, 14
+    )(*early, *late, low, high)
     y_low, y_high = moved(y_last, "gy", 1), moved(y_first, "gy", -1)
     p_box, vx_box, b_box, s_box = call(
         functools.partial(extend, 3, 0), [box] * 4, [SMEM] * 2 + [VMEM] * 7, 3, 20
@@ -403,15 +443,15 @@
     middle, e_first, e_last = call(
         source_middle_kernel,
         [(STEPS, half, tall, layers)]
-        + [(PAIRS * wide + len(late) * (wide + 2 * DEPTH - 2), 8, layers)] * 2,
-        [VMEM] * 7,
+        + [(PAIRS * wide + 4 * (DEPTH - 1), 8, layers)] * 2,
+        [VMEM] * 5,
         3,
         24,
-    )(cells, parts, ends, *late, low2, high2)
+    )(cells, parts, ends, low2, high2)
     e_low, e_high = moved(e_last, "gy", 1), moved(e_first, "gy", -1)
     vy_box, vz_box = call(
-        functools.partial(extend, 2, PAIRS * wide), [box] * 2, [VMEM] * 6, 2, 20
-    )(*late, low2, high2, e_low, e_high)
+        extend_late_kernel, [box] * 2, [VMEM] * 8, 2, 20
+    )(*late, low2, high2, y_low, y_high, e_low, e_high)
     boxes = (p_box, vx_box, vy_box, vz_box, b_box, s_box)
     c_first, c_last = call(
         source_corner_kernel, [(corner_start(PAIRS), 8, layers)] * 2, [VMEM] * 2, 1, 8
@@ -425,7 +465,9 @@
             [VMEM] * 14,
             12,
             32,
-            [pltpu.VMEM(box, jnp.float32)] * 4,
+            [pltpu.VMEM(box, jnp.float32)] * 4
+            + [pltpu.VMEM((4, wide, tall, layers), jnp.float32), pltpu.SemaphoreType.DMA((4, 3))],
+            hbm,
         )(*boxes, ends, middle, s_low, s_high, e_low, e_high, c_low, c_high)
     )
 

time: 193 us -> 196 us (1.016)
  the two profiles are of different devices: /device:TPU:225 before, /device:TPU:206 now
where the time goes in v3:
time: 196 us
  waiting for transfers between devices  108 us (55%)
  starting transfers between devices  53.9 us (28%)
  Pallas kernels  26.7 us (14%)
  local copies, waits for them, and re-layouts  5.05 us (3%)
    all_to_all x1, waiting for transfers between devices, program(): lax.all_to_all(outgoing.reshape(devices, block, 1, layers), ('gx', 'gy'),...  64.5 us
    ppermute x12, waiting for transfers between devices, moved(): return lax.ppermute(block, axis, route)  43.5 us
    ppermute x12, starting transfers between devices, moved(): return lax.ppermute(block, axis, route)  40.5 us
    all_to_all x1, starting transfers between devices, program(): lax.all_to_all(outgoing.reshape(devices, block, 1, layers), ('gx', 'gy'),...  13.4 us
    pallas_call x1, Pallas kernels, program(): call(step_kernel, [(wide, tall, layers)] * 4, [VMEM] * 14, 12, 32, [pltpu...  12.6 us
    unnamed x28, local copies, waits for them, and re-layouts  5.05 us
  transfers between devices with their start and end apart: 13, of which 5 were waited for; matrix products, arithmetic and copies ran while one was open for 0% of the time, Pallas kernels for 6%

profile of v3, /device:TPU:206, one launch (start us, length us, event | category | flops | bytes accessed | tf_op | source)
XLA Modules:
  0.0 195.6 jit_solution(6125016134907332926)
XLA Ops:
  0.6 0.9 convert_reduce_fusion.rank
  1.6 1.2 copy-done.7
  2.8 0.7 copy-done.8
  3.5 0.7 copy-done.9
  4.2 2.3 %shard_map.132 = f32[4352,128]{1,0:T(8,128)S(1)} custom-call(s32[256]{0:T(256)S(1)} %bitcast.9, s32[256]{0:T(256)S(1)} %convert_reduce_fusion.rank, s32[256]{0:T(256)S(1)} %bitcast.10, f32[256,8,128]{2,1,0:T(8,128)S(1)} %bitcast.7), custom_call_target="tpu_custom_call" | custom-call | bytes 6000000 | tf_op jit(solution)/shard_map/pallas_call | solution.py:409
  6.5 1.4 copy-done
  7.8 13.4 %all-to-all-start = ((f32[256,17,1,128]{3,2,1,0:T(1,128)}), f32[256,17,1,128]{3,2,1,0:T(1,128)S(1)}, u32[]{:S(2)}, u32[]{:S(2)}) async-start(f32[256,17,1,128]{3,2,1,0:T(1,128)} %bitcast.6), calls=%async_computation | async-start | bytes 4456448 | tf_op jit(solution)/shard_map/all_to_all | solution.py:412
  21.2 2.5 %shard_map.129 = (f32[3,8,32,128]{3,2,1,0:T(8,128)}, f32[3,8,32,128]{3,2,1,0:T(8,128)}, f32[2,7,32,128]{3,2,1,0:T(8,128)}, f32[2,7,32,128]{3,2,1,0:T(8,128)}) custom-call(f32[32,32,128]{2,1,0:T(8,128)} %refs_2_.1, f32[32,32,128]{2,1,0:T(8,128)} %refs_3_.1, s32[32,32,128]{2,1,0:T(8,128)} %refs_4_.1, f32[32,32,128]{2,1,0:T(8,128)} %vy.5, f32[32,32,128]{2,1,0:T(8,128)} %vz.5), custom_call_target="tpu_custom_call" | custom-call | bytes 2000000 | tf_op jit(solution)/shard_map/pallas_call | solution.py:398
  23.7 2.2 %collective-permute-start = (f32[3,8,32,128]{3,2,1,0:T(8,128)}, f32[3,8,32,128]{3,2,1,0:T(8,128)}, u32[]{:S(2)}, u32[]{:S(2)}) collective-permute-start(f32[3,8,32,128]{3,2,1,0:T(8,128)} %get-tuple-element.26), channel_id=1, source_target_pairs={{0,16},{16,32},{32,48},{48,64},{64,80},{80,96},{96,112},{112,128},... | collective-permute-start | bytes 1179656 | tf_op jit(solution)/shard_map/ppermute | solution.py:44
  25.9 7.4 %collective-permute-start.1 = (f32[3,8,32,128]{3,2,1,0:T(8,128)}, f32[3,8,32,128]{3,2,1,0:T(8,128)}, u32[]{:S(2)}, u32[]{:S(2)}) collective-permute-start(f32[3,8,32,128]{3,2,1,0:T(8,128)} %get-tuple-element.27), channel_id=1, source_target_pairs={{16,0},{32,16},{48,32},{64,48},{80,64},{96,80},{112,96},{128,112},... | collective-permute-start | bytes 1179656 | tf_op jit(solution)/shard_map/ppermute | solution.py:44
  33.3 64.5 %all-to-all-done = f32[256,17,1,128]{3,2,1,0:T(1,128)S(1)} async-done(((f32[256,17,1,128]{3,2,1,0:T(1,128)}), f32[256,17,1,128]{3,2,1,0:T(1,128)S(1)}, u32[]{:S(2)}, u32[]{:S(2)}) %all-to-all-start) | async-done | bytes 2228256 | tf_op jit(solution)/shard_map/all_to_all | solution.py:412
  97.8 3.3 %shard_map.133 = (f32[8,16,32,128]{3,2,1,0:T(8,128)S(1)}, f32[28,32,128]{2,1,0:T(8,128)S(1)}, f32[28,32,128]{2,1,0:T(8,128)S(1)}, f32[8,512]{1,0:T(8,128)S(1)}, bf16[3,512,1024]{2,1,0:T(8,128)(2,1)S(1)}) custom-call(f32[4352,128]{1,0:T(8,128)S(1)} %bitcast.5), custom_call_target="tpu_custom_call" | custom-call | bytes 6000000 | tf_op jit(solution)/shard_map/pallas_call | solution.py:433
  101.1 1.9 collective-permute-start.8
  103.1 1.0 copy-done.5
  104.1 1.3 shard_map.130
  105.4 1.9 collective-permute-start.2
  107.4 1.9 collective-permute-start.4
  109.3 7.6 %collective-permute-start.5 = (f32[2,7,32,128]{3,2,1,0:T(8,128)S(1)}, f32[2,7,32,128]{3,2,1,0:T(8,128)S(1)}, u32[]{:S(2)}, u32[]{:S(2)}) collective-permute-start(f32[2,7,32,128]{3,2,1,0:T(8,128)S(1)} %copy-done.12), channel_id=1, source_target_pairs={{16,0},{32,16},{48,32},{64,48},{80,64},{96,80},{112,96},{128,112},... | collective-permute-start | bytes 688136 | tf_op jit(solution)/shard_map/ppermute | solution.py:44
  116.9 3.9 %collective-permute-start.3 = (f32[208,8,128]{2,1,0:T(8,128)S(1)}, f32[208,8,128]{2,1,0:T(8,128)S(1)}, u32[]{:S(2)}, u32[]{:S(2)}) collective-permute-start(f32[208,8,128]{2,1,0:T(8,128)S(1)} %get-tuple-element.29), channel_id=1, source_target_pairs={{1,0},{2,1},{3,2},{4,3},{5,4},{6,5},{7,6},{8,7},{9,8},{10,9},{11,1... | collective-permute-start | bytes 2555912 | tf_op jit(solution)/shard_map/ppermute | solution.py:44
  120.8 31.9 %collective-permute-done.4.low = f32[2,7,32,128]{3,2,1,0:T(8,128)S(1)} collective-permute-done((f32[2,7,32,128]{3,2,1,0:T(8,128)S(1)}, f32[2,7,32,128]{3,2,1,0:T(8,128)S(1)}, u32[]{:S(2)}, u32[]{:S(2)}) %collective-permute-start.4) | collective-permute-done | bytes 229408 | tf_op jit(solution)/shard_map/ppermute | solution.py:44
  152.7 1.9 collective-permute-start.9
  154.7 2.4 %shard_map.134 = (f32[8,16,32,128]{3,2,1,0:T(8,128)S(1)}, f32[156,8,128]{2,1,0:T(8,128)S(1)}, f32[156,8,128]{2,1,0:T(8,128)S(1)}) custom-call(f32[8,512]{1,0:T(8,128)S(1)} %get-tuple-element.34.cells, bf16[3,512,1024]{2,1,0:T(8,128)(2,1)S(1)} %get-tuple-element.35.parts, f32[8,16,32,128]{3,2,1,0:T(8,128)S(1)} %get-tuple-element.36.ends, ...), custom_call_target="tpu_custom_call" | custom-call | bytes 6000000 | tf_op jit(solution)/shard_map/pallas_call | solution.py:443
  157.1 1.9 collective-permute-start.6
  159.1 3.9 %collective-permute-start.7 = (f32[156,8,128]{2,1,0:T(8,128)S(1)}, f32[156,8,128]{2,1,0:T(8,128)S(1)}, u32[]{:S(2)}, u32[]{:S(2)}) collective-permute-start(f32[156,8,128]{2,1,0:T(8,128)S(1)} %get-tuple-element.38), channel_id=1, source_target_pairs={{1,0},{2,1},{3,2},{4,3},{5,4},{6,5},{7,6},{8,7},{9,8},{10,9},{11,1... | collective-permute-start | bytes 1916936 | tf_op jit(solution)/shard_map/ppermute | solution.py:44
  163.0 4.0 %collective-permute-start.10 = (f32[36,8,128]{2,1,0:T(8,128)S(1)}, f32[36,8,128]{2,1,0:T(8,128)S(1)}, u32[]{:S(2)}, u32[]{:S(2)}) collective-permute-start(f32[36,8,128]{2,1,0:T(8,128)S(1)} %get-tuple-element.46), channel_id=1, source_target_pairs={{0,1},{1,2},{2,3},{3,4},{4,5},{5,6},{6,7},{7,8},{8,9},{9,10},{10,1... | collective-permute-start | bytes 442376 | tf_op jit(solution)/shard_map/ppermute | solution.py:44
  167.1 1.9 collective-permute-start.11
  169.1 2.1 %shard_map.131 = (f32[48,48,128]{2,1,0:T(8,128)S(1)}, f32[48,48,128]{2,1,0:T(8,128)S(1)}, f32[48,48,128]{2,1,0:T(8,128)S(1)}, f32[48,48,128]{2,1,0:T(8,128)S(1)}) custom-call(f32[4]{0:T(128)S(1)} %get-tuple-element.49.refs_0_, f32[4]{0:T(128)S(1)} %get-tuple-element.48.refs_1_, f32[32,32,128]{2,1,0:T(8,128)S(1)} %copy-done.1, f32[32,32,128]{2,1,0:T(8,128)S(1)} %copy-done.2, ...), custom_call_target="tpu_custom_call" | custom-call | bytes 6000000 | tf_op jit(solution)/shard_map/pallas_call | solution.py:428
  171.2 5.1 %collective-permute-done.6.elow.ylow = f32[156,8,128]{2,1,0:T(8,128)S(1)} collective-permute-done((f32[156,8,128]{2,1,0:T(8,128)S(1)}, f32[156,8,128]{2,1,0:T(8,128)S(1)}, u32[]{:S(2)}, u32[]{:S(2)}) %collective-permute-start.6) | collective-permute-done | bytes 639008 | tf_op jit(solution)/shard_map/ppermute | solution.py:44
  176.3 4.0 %collective-permute-done.7.ehigh.yhigh = f32[156,8,128]{2,1,0:T(8,128)S(1)} collective-permute-done((f32[156,8,128]{2,1,0:T(8,128)S(1)}, f32[156,8,128]{2,1,0:T(8,128)S(1)}, u32[]{:S(2)}, u32[]{:S(2)}) %collective-permute-start.7) | collective-permute-done | bytes 639008 | tf_op jit(solution)/shard_map/ppermute | solution.py:44
  180.3 0.3 shard_map.135
  180.6 2.4 %collective-permute-done.11.chigh = f32[36,8,128]{2,1,0:T(8,128)S(1)} collective-permute-done((f32[36,8,128]{2,1,0:T(8,128)S(1)}, f32[36,8,128]{2,1,0:T(8,128)S(1)}, u32[]{:S(2)}, u32[]{:S(2)}) %collective-permute-start.11) | collective-permute-done | bytes 147488 | tf_op jit(solution)/shard_map/ppermute | solution.py:44
  183.0 12.6 %shard_map.137 = (f32[32,32,128]{2,1,0:T(8,128)}, f32[32,32,128]{2,1,0:T(8,128)}, f32[32,32,128]{2,1,0:T(8,128)}, f32[32,32,128]{2,1,0:T(8,128)}) custom-call(f32[48,48,128]{2,1,0:T(8,128)S(1)} %get-tuple-element.30.p0, f32[48,48,128]{2,1,0:T(8,128)S(1)} %get-tuple-element.31.vx0, f32[48,48,128]{2,1,0:T(8,128)S(1)} %get-tuple-element.39.vy0, ...), custom_call_target="tpu_custom_call" | custom-call | bytes 24000000 | tf_op jit(solution)/shard_map/pallas_call | solution.py:462
  (33 shorter events, 0.1 us)
Async XLA Ops:
  1.6 1.2 copy-start.7
  2.8 0.7 copy-start.8
  3.5 0.7 copy-start.9
  6.5 1.4 copy-start
  7.8 90.0 %all-to-all-start = ((f32[256,17,1,128]{3,2,1,0:T(1,128)}), f32[256,17,1,128]{3,2,1,0:T(1,128)S(1)}, u32[]{:S(2)}, u32[]{:S(2)}) async-start(f32[256,17,1,128]{3,2,1,0:T(1,128)} %bitcast.6), calls=%async_computation | async-start | bytes 4456448 | tf_op jit(solution)/shard_map/all_to_all | solution.py:412
  23.7 79.4 %copy-start.1 = (f32[32,32,128]{2,1,0:T(8,128)S(1)}, f32[32,32,128]{2,1,0:T(8,128)}, u32[]{:S(2)}) copy-start(f32[32,32,128]{2,1,0:T(8,128)} %refs_2_.1) | copy-start | bytes 1572868
  23.7 79.4 %copy-start.2 = (f32[32,32,128]{2,1,0:T(8,128)S(1)}, f32[32,32,128]{2,1,0:T(8,128)}, u32[]{:S(2)}) copy-start(f32[32,32,128]{2,1,0:T(8,128)} %refs_3_.1) | copy-start | bytes 1572868
  23.7 79.3 %collective-permute-start = (f32[3,8,32,128]{3,2,1,0:T(8,128)}, f32[3,8,32,128]{3,2,1,0:T(8,128)}, u32[]{:S(2)}, u32[]{:S(2)}) collective-permute-start(f32[3,8,32,128]{3,2,1,0:T(8,128)} %get-tuple-element.26), channel_id=1, source_target_pairs={{0,16},{16,32},{32,48},{48,64},{64,80},{80,96},{96,112},{112,128},... | collective-permute-start | bytes 1179656 | tf_op jit(solution)/shard_map/ppermute | solution.py:44
  25.9 77.2 %collective-permute-start.1 = (f32[3,8,32,128]{3,2,1,0:T(8,128)}, f32[3,8,32,128]{3,2,1,0:T(8,128)}, u32[]{:S(2)}, u32[]{:S(2)}) collective-permute-start(f32[3,8,32,128]{3,2,1,0:T(8,128)} %get-tuple-element.27), channel_id=1, source_target_pairs={{16,0},{32,16},{48,32},{64,48},{80,64},{96,80},{112,96},{128,112},... | collective-permute-start | bytes 1179656 | tf_op jit(solution)/shard_map/ppermute | solution.py:44
  97.8 5.3 %copy-start.3 = (s32[32,32,128]{2,1,0:T(8,128)S(1)}, s32[32,32,128]{2,1,0:T(8,128)}, u32[]{:S(2)}) copy-start(s32[32,32,128]{2,1,0:T(8,128)} %refs_4_.1) | copy-start | bytes 1572868
  97.8 5.3 %copy-start.4 = (f32[32,32,128]{2,1,0:T(8,128)S(1)}, f32[32,32,128]{2,1,0:T(8,128)}, u32[]{:S(2)}) copy-start(f32[32,32,128]{2,1,0:T(8,128)} %vy.5) | copy-start | bytes 1572868
  101.1 58.0 %collective-permute-start.8 = (f32[28,32,128]{2,1,0:T(8,128)S(1)}, f32[28,32,128]{2,1,0:T(8,128)S(1)}, u32[]{:S(2)}, u32[]{:S(2)}) collective-permute-start(f32[28,32,128]{2,1,0:T(8,128)S(1)} %get-tuple-element.44), channel_id=1, source_target_pairs={{0,16},{16,32},{32,48},{48,64},{64,80},{80,96},{96,112},{112,128},... | collective-permute-start | bytes 1376264 | tf_op jit(solution)/shard_map/ppermute | solution.py:44
  103.1 1.0 copy-start.5
  104.1 3.2 %copy-start.13 = (f32[2,7,32,128]{3,2,1,0:T(8,128)S(1)}, f32[2,7,32,128]{3,2,1,0:T(8,128)}, u32[]{:S(2)}) copy-start(f32[2,7,32,128]{3,2,1,0:T(8,128)} %get-tuple-element.32) | copy-start | bytes 688132
  104.1 5.2 %copy-start.12 = (f32[2,7,32,128]{3,2,1,0:T(8,128)S(1)}, f32[2,7,32,128]{3,2,1,0:T(8,128)}, u32[]{:S(2)}) copy-start(f32[2,7,32,128]{3,2,1,0:T(8,128)} %get-tuple-element.33) | copy-start | bytes 688132
  105.4 61.6 %collective-permute-start.2 = (f32[208,8,128]{2,1,0:T(8,128)S(1)}, f32[208,8,128]{2,1,0:T(8,128)S(1)}, u32[]{:S(2)}, u32[]{:S(2)}) collective-permute-start(f32[208,8,128]{2,1,0:T(8,128)S(1)} %get-tuple-element.28), channel_id=1, source_target_pairs={{0,1},{1,2},{2,3},{3,4},{4,5},{5,6},{6,7},{7,8},{8,9},{9,10},{10,1... | collective-permute-start | bytes 2555912 | tf_op jit(solution)/shard_map/ppermute | solution.py:44
  107.4 45.4 %collective-permute-start.4 = (f32[2,7,32,128]{3,2,1,0:T(8,128)S(1)}, f32[2,7,32,128]{3,2,1,0:T(8,128)S(1)}, u32[]{:S(2)}, u32[]{:S(2)}) collective-permute-start(f32[2,7,32,128]{3,2,1,0:T(8,128)S(1)} %copy-done.13), channel_id=1, source_target_pairs={{0,16},{16,32},{32,48},{48,64},{64,80},{80,96},{96,112},{112,128},... | collective-permute-start | bytes 688136 | tf_op jit(solution)/shard_map/ppermute | solution.py:44
  109.3 45.3 %collective-permute-start.5 = (f32[2,7,32,128]{3,2,1,0:T(8,128)S(1)}, f32[2,7,32,128]{3,2,1,0:T(8,128)S(1)}, u32[]{:S(2)}, u32[]{:S(2)}) collective-permute-start(f32[2,7,32,128]{3,2,1,0:T(8,128)S(1)} %copy-done.12), channel_id=1, source_target_pairs={{16,0},{32,16},{48,32},{64,48},{80,64},{96,80},{112,96},{128,112},... | collective-permute-start | bytes 688136 | tf_op jit(solution)/shard_map/ppermute | solution.py:44
  116.9 52.2 %collective-permute-start.3 = (f32[208,8,128]{2,1,0:T(8,128)S(1)}, f32[208,8,128]{2,1,0:T(8,128)S(1)}, u32[]{:S(2)}, u32[]{:S(2)}) collective-permute-start(f32[208,8,128]{2,1,0:T(8,128)S(1)} %get-tuple-element.29), channel_id=1, source_target_pairs={{1,0},{2,1},{3,2},{4,3},{5,4},{6,5},{7,6},{8,7},{9,8},{10,9},{11,1... | collective-permute-start | bytes 2555912 | tf_op jit(solution)/shard_map/ppermute | solution.py:44
  152.7 10.3 %collective-permute-start.9 = (f32[28,32,128]{2,1,0:T(8,128)S(1)}, f32[28,32,128]{2,1,0:T(8,128)S(1)}, u32[]{:S(2)}, u32[]{:S(2)}) collective-permute-start(f32[28,32,128]{2,1,0:T(8,128)S(1)} %get-tuple-element.45), channel_id=1, source_target_pairs={{16,0},{32,16},{48,32},{64,48},{80,64},{96,80},{112,96},{128,112},... | collective-permute-start | bytes 1376264 | tf_op jit(solution)/shard_map/ppermute | solution.py:44
  154.7 14.4 %copy-start.10 = (f32[4]{0:T(128)S(1)}, f32[4]{0:T(128)}, u32[]{:S(2)}) copy-start(f32[4]{0:T(128)} %param.16) | copy-start | bytes 52
  154.7 14.4 %copy-start.11 = (f32[4]{0:T(128)S(1)}, f32[4]{0:T(128)}, u32[]{:S(2)}) copy-start(f32[4]{0:T(128)} %param.15) | copy-start | bytes 52
  157.1 19.1 %collective-permute-start.6 = (f32[156,8,128]{2,1,0:T(8,128)S(1)}, f32[156,8,128]{2,1,0:T(8,128)S(1)}, u32[]{:S(2)}, u32[]{:S(2)}) collective-permute-start(f32[156,8,128]{2,1,0:T(8,128)S(1)} %get-tuple-element.37), channel_id=1, source_target_pairs={{0,1},{1,2},{2,3},{3,4},{4,5},{5,6},{6,7},{7,8},{8,9},{9,10},{10,1... | collective-permute-start | bytes 1916936 | tf_op jit(solution)/shard_map/ppermute | solution.py:44
  159.1 21.3 %collective-permute-start.7 = (f32[156,8,128]{2,1,0:T(8,128)S(1)}, f32[156,8,128]{2,1,0:T(8,128)S(1)}, u32[]{:S(2)}, u32[]{:S(2)}) collective-permute-start(f32[156,8,128]{2,1,0:T(8,128)S(1)} %get-tuple-element.38), channel_id=1, source_target_pairs={{1,0},{2,1},{3,2},{4,3},{5,4},{6,5},{7,6},{8,7},{9,8},{10,9},{11,1... | collective-permute-start | bytes 1916936 | tf_op jit(solution)/shard_map/ppermute | solution.py:44
  163.0 17.6 %collective-permute-start.10 = (f32[36,8,128]{2,1,0:T(8,128)S(1)}, f32[36,8,128]{2,1,0:T(8,128)S(1)}, u32[]{:S(2)}, u32[]{:S(2)}) collective-permute-start(f32[36,8,128]{2,1,0:T(8,128)S(1)} %get-tuple-element.46), channel_id=1, source_target_pairs={{0,1},{1,2},{2,3},{3,4},{4,5},{5,6},{6,7},{7,8},{8,9},{9,10},{10,1... | collective-permute-start | bytes 442376 | tf_op jit(solution)/shard_map/ppermute | solution.py:44
  167.1 15.9 %collective-permute-start.11 = (f32[36,8,128]{2,1,0:T(8,128)S(1)}, f32[36,8,128]{2,1,0:T(8,128)S(1)}, u32[]{:S(2)}, u32[]{:S(2)}) collective-permute-start(f32[36,8,128]{2,1,0:T(8,128)S(1)} %get-tuple-element.47), channel_id=1, source_target_pairs={{1,0},{2,1},{3,2},{4,3},{5,4},{6,5},{7,6},{8,7},{9,8},{10,9},{11,1... | collective-permute-start | bytes 442376 | tf_op jit(solution)/shard_map/ppermute | solution.py:44
  169.1 11.3 %copy-start.6 = (f32[32,32,128]{2,1,0:T(8,128)S(1)}, f32[32,32,128]{2,1,0:T(8,128)}, u32[]{:S(2)}) copy-start(f32[32,32,128]{2,1,0:T(8,128)} %vz.5) | copy-start | bytes 1572868
